TPU v7x, 256 devices: a whole 4x4x8 slice. The times are simulated.
256 devices in a mesh: sim: 64 (over x, y_lo, z), grp: 4 (over y_hi, core).
Axes of the slice: x: 4, y: 4 (y_hi: 2, y_lo: 2; y = y_hi * 2 + y_lo), z: 8, core: 2. Of those that a mesh axis runs over, the one named last changes fastest.
Arguments:
- velocity: float32 [64, 4, 3, 256, 512], P('sim', 'grp'), may hold values from -6 to 6
- slot_of: int32 [64, 4, 256], P('sim', 'grp'), may hold values from 0 to 255, each once within a row
- w_encode: bfloat16 [1024, 256], replicated, may hold values from -0.1875 to 0.1875
- w_conv: bfloat16 [27, 256, 256], replicated, may hold values from -0.078125 to 0.078125
- w_head: bfloat16 [256, 128], replicated, may hold values from -0.375 to 0.375
Outputs:
- velocity_next: float32 [64, 4, 3, 256, 512], P('sim', 'grp')
- grad_encode: float32 [1024, 256], P(None, 'grp')
- grad_conv: float32 [27, 256, 256], P(None, None, 'grp')
- grad_head: float32 [256, 128], P('grp')
Inputs may be any that keep to these rules, and one draw needn't show every extreme that they name: `slot_of`: each block's row of 256 entries names every slot once.
All inputs are finite; a program needn't handle non-finite values.
Results may differ from a plain program's by a relative error of at most 0.0085.
Values may be sent and summed in bfloat16 or wider, within the bound.
A program may use at most 128 MiB of HBM per device.

v0:
```python
import jax
import jax.numpy as jnp
import numpy as np
from jax import lax
from jax.sharding import PartitionSpec as P

NP = 8
EX = 2
EY = 4
EZ = 32
STEPS = 2


VISCOSITY = 0.2
TIME_STEP = 0.005
PENALTY = 100.0
LOSS_WEIGHT = 64.0


def as_sent(value):

    def short(part):
        return part.astype(jnp.bfloat16) if part.dtype == jnp.float32 else part

    return jax.tree.map(short, value)


def passed_along(value, axis, steps):
    count = lax.axis_size(axis)
    pairs = [(source, (source + steps) % count) for source in range(count)]
    return lax.ppermute(value, axis, pairs)


def from_behind(block, axis, distance):
    devices = range(lax.axis_size(axis))
    route = [(i - distance, i) for i in devices if i - distance in devices]
    return lax.ppermute(block, axis, route)


def derivative_matrix(count):
    places = np.arange(count)
    points = -np.cos(np.pi * places / (count - 1))
    weights = np.where(places % 2 == 0, 1.0, -1.0)
    weights[0] = weights[0] * 0.5
    weights[count - 1] = weights[count - 1] * 0.5
    identity = np.eye(count)
    spread = points[:, None] - points[None, :] + identity
    deriv = weights[None, :] / weights[:, None] / spread
    deriv = deriv * (1.0 - identity)
    return deriv - identity * deriv.sum(axis=1)[:, None]


def element_tables(count):
    deriv = derivative_matrix(count)
    single = np.eye(count)
    square = np.eye(count * count)
    along_x = np.kron(deriv, square)
    along_y = np.kron(single, np.kron(deriv, single))
    along_z = np.kron(square, deriv)
    laplace = along_x @ along_x + along_y @ along_y + along_z @ along_z
    stencil = np.concatenate([along_x.T, along_y.T, along_z.T, laplace.T], axis=1)
    grid = np.arange(count**3).reshape(count, count, count)
    final = count - 1
    chosen = np.concatenate(
        [
            grid[0].ravel(),
            grid[final].ravel(),
            grid[:, 0].ravel(),
            grid[:, final].ravel(),
            grid[:, :, 0].ravel(),
            grid[:, :, final].ravel(),
        ]
    )
    select = np.zeros((count**3, chosen.size))
    select[chosen, np.arange(chosen.size)] = 1.0
    bottom = np.zeros((count**3, count * count))
    for first in range(count):
        for middle in range(count):
            for inner in range(count):
                bottom[grid[first, middle, inner], first * count + inner] = (
                    VISCOSITY * deriv[0, middle]
                )
    return (
        jnp.asarray(stencil, jnp.float32),
        jnp.asarray(select, jnp.float32),
        jnp.asarray(bottom, jnp.float32),
    )


def silu_grad(value):
    sigma = jax.nn.sigmoid(value)
    return sigma * (1.0 + value * (1.0 - sigma))


def advance(field, faces, beside, stencil, select):
    points = field.shape[-1]
    derived = jnp.einsum("cxyzp,pq->cxyzq", field, stencil, precision=lax.Precision.HIGHEST)
    advect = field[0][None] * derived[..., 0:points]
    advect = advect + field[1][None] * derived[..., points : 2 * points]
    advect = advect + field[2][None] * derived[..., 2 * points : 3 * points]
    laplace = derived[..., 3 * points :]
    penalty = jnp.einsum("cxyzq,pq->cxyzp", beside - faces, select, precision=lax.Precision.HIGHEST)
    return field + TIME_STEP * (VISCOSITY * (laplace + PENALTY * penalty) - advect)


def face_part(faces, which):
    width = faces.shape[-1] // 6
    return faces[..., which * width : (which + 1) * width]


def local_beside(faces):
    last_x = face_part(faces, 1)[:, -1]
    from_left = passed_along(as_sent(last_x.reshape(3, -1)), "sim", 1).reshape(last_x.shape)
    first_x = face_part(faces, 0)[:, 0]
    from_right = passed_along(as_sent(first_x.reshape(3, -1)), "sim", -1).reshape(first_x.shape)
    before_x = jnp.concatenate([from_left[:, None], face_part(faces, 1)[:, :-1]], axis=1)
    after_x = jnp.concatenate([face_part(faces, 0)[:, 1:], from_right[:, None]], axis=1)
    top_y = face_part(faces, 3)[:, :, -1]
    from_below = from_behind(as_sent(top_y.reshape(3, -1)), "grp", 1).reshape(top_y.shape)
    base_y = face_part(faces, 2)[:, :, 0]
    from_above = from_behind(as_sent(base_y.reshape(3, -1)), "grp", -1).reshape(base_y.shape)
    below = jnp.concatenate([from_below[:, :, None], face_part(faces, 3)[:, :, :-1]], axis=2)
    above = jnp.concatenate([face_part(faces, 2)[:, :, 1:], from_above[:, :, None]], axis=2)
    before_z = jnp.roll(face_part(faces, 5), 1, axis=3)
    after_z = jnp.roll(face_part(faces, 4), -1, axis=3)
    return jnp.concatenate([before_x, after_x, below, above, before_z, after_z], axis=-1)


def crop_windows(grid, sign):
    padded = jnp.pad(grid, ((1, 1), (1, 1), (1, 1), (0, 0)))
    lengths = grid.shape[:3]
    pieces = []
    for shift_x in (-1, 0, 1):
        for shift_y in (-1, 0, 1):
            for shift_z in (-1, 0, 1):
                start_x = 1 + sign * shift_x
                start_y = 1 + sign * shift_y
                start_z = 1 + sign * shift_z
                pieces.append(
                    padded[
                        start_x : start_x + lengths[0],
                        start_y : start_y + lengths[1],
                        start_z : start_z + lengths[2],
                    ]
                )
    return jnp.concatenate(pieces, axis=-1).reshape(-1, 27 * grid.shape[-1])


def train_core(h1_grid, target_rows, w_conv, w_head, total):
    channels = h1_grid.shape[-1]
    patches = crop_windows(h1_grid, 1)
    z2 = jnp.dot(
        patches, w_conv.reshape(27 * channels, channels), preferred_element_type=jnp.float32
    )
    h2 = jax.nn.silu(z2).astype(jnp.bfloat16)
    output = jnp.dot(h2, w_head, preferred_element_type=jnp.float32)
    resid = (LOSS_WEIGHT * (output - target_rows.astype(jnp.float32)) / total).astype(jnp.bfloat16)
    grad_head = jnp.einsum("nc,no->co", h2, resid, preferred_element_type=jnp.float32)
    dh2 = jnp.dot(resid, w_head.T, preferred_element_type=jnp.float32)
    dz2 = (dh2 * silu_grad(z2)).astype(jnp.bfloat16)
    grad_conv = jnp.einsum("nk,nc->kc", patches, dz2, preferred_element_type=jnp.float32).reshape(
        27, channels, channels
    )
    back_patches = crop_windows(dz2.reshape(h1_grid.shape), -1)
    flipped = jnp.transpose(w_conv, (0, 2, 1)).reshape(27 * channels, channels)
    dh1 = jnp.dot(back_patches, flipped, preferred_element_type=jnp.float32)
    return (dh1, grad_conv, grad_head)


def body(velocity, slot_of, w_encode, w_conv, w_head):
    stencil, select, bottom = element_tables(NP)
    block = velocity[0, 0]
    slots = slot_of[0, 0]
    points = block.shape[-1]
    field = block[:, slots].reshape(3, EX, EY, EZ, points)
    for step in range(STEPS):
        faces = jnp.einsum("cxyzp,pq->cxyzq", field, select, precision=lax.Precision.HIGHEST)
        beside = local_beside(faces)
        field = advance(field, faces, beside, stencil, select)
    inverse = jnp.argsort(slots)
    velocity_next = field.reshape(3, EX * EY * EZ, points)[:, inverse][None, None]
    snapshot = jnp.concatenate([field[0], field[2]], axis=-1).astype(jnp.bfloat16)
    wall_low = jnp.einsum("xyzp,pq->xyzq", field[0], bottom, precision=lax.Precision.HIGHEST)
    wall_side = jnp.einsum("xyzp,pq->xyzq", field[2], bottom, precision=lax.Precision.HIGHEST)
    target = jnp.concatenate([wall_low, wall_side], axis=-1).astype(jnp.bfloat16)
    groups = lax.axis_size("grp")
    total = EX * EY * EZ * lax.axis_size("sim") * groups
    crop_x, crop_t = (
        lax.all_to_all(snapshot, "grp", split_axis=2, concat_axis=1, tiled=True),
        lax.all_to_all(target, "grp", split_axis=2, concat_axis=1, tiled=True),
    )
    rows = crop_x.reshape(-1, crop_x.shape[-1])
    z1 = jnp.dot(rows, w_encode, preferred_element_type=jnp.float32)
    h1 = jax.nn.silu(z1).astype(jnp.bfloat16)
    dh1, grad_conv, grad_head = train_core(
        h1.reshape(crop_x.shape[:3] + (h1.shape[-1],)),
        crop_t.reshape(-1, crop_t.shape[-1]),
        w_conv,
        w_head,
        total,
    )
    dz1 = (dh1 * silu_grad(z1)).astype(jnp.bfloat16)
    grad_encode = jnp.einsum("nf,nc->fc", rows, dz1, preferred_element_type=jnp.float32)
    total_encode, total_conv, total_head = lax.psum(
        (grad_encode, grad_conv, grad_head), ("sim", "grp")
    )
    quarter = w_encode.shape[1] // groups
    start = lax.axis_index("grp") * quarter
    out_encode = lax.dynamic_slice_in_dim(total_encode, start, quarter, 1)
    out_conv = lax.dynamic_slice_in_dim(total_conv, start, quarter, 2)
    out_head = lax.dynamic_slice_in_dim(total_head, start, quarter, 0)
    return (velocity_next, out_encode, out_conv, out_head)


def solution(mesh):
    placed = (P("sim", "grp", None, None, None), P("sim", "grp", None), P(), P(), P())
    return jax.shard_map(
        body,
        mesh=mesh,
        in_specs=placed,
        out_specs=(
            P("sim", "grp", None, None, None),
            P(None, "grp"),
            P(None, None, "grp"),
            P("grp", None),
        ),
        check_vma=False,
    )
```

profile of v0, /device:TPU:24, one launch (start us, length us, event | category | flops | bytes accessed | tf_op | source)
XLA Modules:
  0.0 504.7 jit_solution(17894706739257734148)
XLA Ops:
  7.2 2.6 copy.56
  9.8 3.2 sort.17
  13.0 3.1 gather_fusion
  16.0 2.1 copy.35
  18.1 4.3 fusion.42
  24.1 1.9 collective-permute-start
  26.2 4.2 collective-permute-start.1
  32.0 1.9 collective-permute-start.2
  34.6 5.9 %collective-permute-start.3 = (bf16[3,4096]{1,0:T(4,128)(2,1)}, bf16[3,4096]{1,0:T(4,128)(2,1)}, u32[]{:S(2)}, u32[]{:S(2)}) collective-permute-start(bf16[3,4096]{1,0:T(4,128)(2,1)} %convert_element_type.185), channel_id=1, source_target_pairs={{1,0},{2,1},{3,2},{5,4},{6,5},{7,6},{9,8},{10,9},{11,10},{13,12},{... | collective-permute-start | bytes 73736 | tf_op jit(solution)/shard_map/ppermute | solution.py:37
  42.5 4.4 fusion.29
  46.9 12.2 %fusion.44 = f32[3,2,4,32,2048]{4,3,2,1,0:T(8,128)} fusion(f32[3,2,4,32,512]{4,3,2,1,0:T(8,128)S(1)} %bitcast.158, f32[512,2048,1,1,1]{1,0,4,3,2:T(8,128)S(1)} %copy-done.2), kind=kOutput, calls=%fused_computation.197 | convolution fusion | flops 9663676416 | bytes 12058624 | tf_op jit(solution)/shard_map/cxyzp,pq->cxyzq/dot_general | solution.py:97
  65.2 1.6 reshape.257
  66.8 1.8 pad_maximum_fusion.1
  68.7 1.6 reshape.258
  70.3 1.7 pad_maximum_fusion.2
  72.1 2.3 concatenate.170
  74.3 7.5 %fusion.9 = f32[3,2,4,32,512]{4,3,2,1,0:T(8,128)S(1)} fusion(f32[3,2,4,32,512]{4,3,2,1,0:T(8,128)} %bitcast.159, f32[3,2,4,32,2048]{4,3,2,1,0:T(8,128)} %fusion.44, f32[512,384,1,1,1]{1,0,4,3,2:T(8,128)} %constant.46, f32[3,2,4,32,384]{4,3,2,1,0:T(8,128)} %concatenate.170, f32[3,2,4,32,384]{4,3,2,1,0:T(8,128)S(1)} %get-tuple-element.106, ...), kind=kOutput, calls=%fused_computation.69 | convolution fusion | flops 1816559616 | bytes 14155776 | tf_op jit(solution)/shard_map/cxyzq,pq->cxyzp/dot_general | solution.py:102
  81.9 12.3 %fusion.45 = f32[3,2,4,32,2048]{4,3,2,1,0:T(8,128)} fusion(f32[3,2,4,32,512]{4,3,2,1,0:T(8,128)S(1)} %fusion.9, f32[512,2048,1,1,1]{1,0,4,3,2:T(8,128)S(1)} %copy-done.3), kind=kOutput, calls=%fused_computation.198 | convolution fusion | flops 9663676416 | bytes 12058624 | tf_op jit(solution)/shard_map/cxyzp,pq->cxyzq/dot_general | solution.py:97
  94.2 2.6 fusion.43
  102.4 1.6 convert_element_type.188
  104.0 1.6 convert_element_type.191
  105.6 4.1 collective-permute-start.5
  109.8 1.5 convert_element_type.194
  111.3 1.9 collective-permute-start.6
  113.9 5.1 %collective-permute-start.7 = (bf16[3,4096]{1,0:T(4,128)(2,1)}, bf16[3,4096]{1,0:T(4,128)(2,1)S(1)}, u32[]{:S(2)}, u32[]{:S(2)}) collective-permute-start(bf16[3,4096]{1,0:T(4,128)(2,1)} %convert_element_type.197), channel_id=1, source_target_pairs={{1,0},{2,1},{3,2},{5,4},{6,5},{7,6},{9,8},{10,9},{11,10},{13,12},{... | collective-permute-start | bytes 73736 | tf_op jit(solution)/shard_map/ppermute | solution.py:37
  119.0 1.9 pad_maximum_fusion.11
  120.9 1.9 pad_maximum_fusion.12
  124.3 1.8 pad_maximum_fusion.9
  126.8 1.8 pad_maximum_fusion.10
  128.7 1.6 reshape.261
  130.3 1.8 pad_maximum_fusion.7
  132.1 1.6 reshape.262
  133.8 1.7 pad_maximum_fusion.8
  135.5 2.9 concatenate.177
  138.4 7.0 %fusion.3 = f32[3,2,4,32,512]{4,3,2,1,0:T(8,128)S(1)} fusion(f32[3,2,4,32,512]{4,3,2,1,0:T(8,128)S(1)} %fusion.9, f32[3,2,4,32,2048]{4,3,2,1,0:T(8,128)} %fusion.45, f32[512,384,1,1,1]{1,0,4,3,2:T(8,128)} %constant.46, f32[3,2,4,32,384]{4,3,2,1,0:T(8,128)} %concatenate.177, f32[3,2,4,32,384]{4,3,2,1,0:T(8,128)S(1)} %get-tuple-element.108, ...), kind=kOutput, calls=%fused_computation.59 | convolution fusion | flops 1816559616 | bytes 14155776 | tf_op jit(solution)/shard_map/cxyzq,pq->cxyzp/dot_general | solution.py:102
  147.9 4.8 all-to-all-start.1
  154.9 6.8 %all-to-all-start = ((bf16[2,4,32,1024]{3,1,0,2:T(4,128)(2,1)}), bf16[2,4,32,1024]{3,1,0,2:T(4,128)(2,1)S(1)}, u32[]{:S(2)}, u32[]{:S(2)}) async-start(bf16[2,4,32,1024]{3,1,0,2:T(4,128)(2,1)} %copy.37), calls=%async_computation | async-start | bytes 1048576 | tf_op jit(solution)/shard_map/all_to_all | solution.py:189
  161.7 5.7 %copy.42 = bf16[27,256,256]{1,2,0:T(8,128)(2,1)} copy(bf16[27,256,256]{2,1,0:T(8,128)(2,1)} %param.11) | data formatting | bytes 7077888 | tf_op args[3]
  170.4 2.7 copy-done.8
  185.5 6.0 %copy.43 = bf16[6912,256]{1,0:T(8,128)(2,1)} copy(bf16[6912,256]{0,1:T(8,128)(2,1)} %bitcast.169) | data formatting | bytes 7077888 | tf_op jit(solution)/shard_map/nk,nc->kc/dot_general | solution.py:161
  191.4 6.0 %fusion.25 = f32[27,256,256]{1,2,0:T(8,128)} fusion(bf16[27,256,256]{2,1,0:T(8,128)(2,1)} %bitcast.161, bf16[256,256]{1,0:T(8,128)(2,1)S(1)} %fusion.14), kind=kOutput, calls=%fused_computation.116 | convolution fusion | flops 905969664 | bytes 10747904 | tf_op jit(solution)/shard_map/nk,nc->kc/dot_general | solution.py:161
  206.3 5.7 %fusion.16 = f32[1024,256]{0,1:T(8,128)} fusion(bf16[256,1024]{1,0:T(8,128)(2,1)S(1)} %bitcast.217, bf16[256,6912]{1,0:T(8,128)(2,1)} %constant_dynamic-update-slice_fusion.27, bf16[6912,256]{1,0:T(8,128)(2,1)} %bitcast.171, f32[256,256]{1,0:T(8,128)S(1)} %get-tuple-element.110), kind=kOutput, calls=%fused_computation.81 | convolution fusion | flops 1040777216 | bytes 8912896 | tf_op jit(solution)/shard_map/nf,nc->fc/dot_general | solution.py:203
  213.4 2.4 copy.36
  215.8 3.4 gather_fusion.1
  219.2 1.6 copy.45
  220.9 270.8 %all-reduce.5.cloned.1.call-done = (f32[1024,256]{0,1:T(8,128)}, f32[27,256,256]{1,2,0:T(8,128)}, f32[256,128]{1,0:T(8,128)}) async-done(((f32[1024,256]{0,1:T(8,128)}, f32[27,256,256]{1,2,0:T(8,128)}, f32[256,128]{1,0:T(8,128)}), (f32[1024,256]{0,1:T(8,128)}, f32[27,256,256]{1,2,0:T(8,128)}, f32[256,128]{1,0:T(8,128)})) %all-reduce.5.cloned.1.call-update) | async-done | bytes 8257552 | tf_op jit(solution)/shard_map/psum | solution.py:204
  491.7 1.7 constant_dynamic-slice_fusion.2
  493.4 2.9 constant_dynamic-slice_fusion.1
  (147 shorter events, 52.0 us)
Async XLA Ops:
  7.2 162.1 %copy-start = (bf16[1024,256]{1,0:T(8,128)(2,1)S(1)}, bf16[1024,256]{1,0:T(8,128)(2,1)}, u32[]{:S(2)}) copy-start(bf16[1024,256]{1,0:T(8,128)(2,1)} %param.10) | copy-start | bytes 1572868
  7.2 2.6 copy-start.13
  18.1 28.8 %copy-start.1 = (f32[3,256,512]{2,1,0:T(8,128)}, f32[3,256,512]{2,1,0:T(8,128)S(1)}, u32[]{:S(2)}) copy-start(f32[3,256,512]{2,1,0:T(8,128)S(1)} %copy.35) | copy-start | bytes 4718596
  22.5 0.8 copy-start.9
  24.1 41.1 %collective-permute-start = (bf16[3,8192]{1,0:T(4,128)(2,1)}, bf16[3,8192]{1,0:T(4,128)(2,1)}, u32[]{:S(2)}, u32[]{:S(2)}) collective-permute-start(bf16[3,8192]{1,0:T(4,128)(2,1)} %convert_element_type.176), channel_id=1, source_target_pairs={{0,4},{4,8},{8,12},{12,16},{16,20},{20,24},{24,28},{28,32},{32,36}... | collective-permute-start | bytes 147464 | tf_op jit(solution)/shard_map/ppermute | solution.py:31
  26.2 42.5 %collective-permute-start.1 = (bf16[3,8192]{1,0:T(4,128)(2,1)S(1)}, bf16[3,8192]{1,0:T(4,128)(2,1)}, u32[]{:S(2)}, u32[]{:S(2)}) collective-permute-start(bf16[3,8192]{1,0:T(4,128)(2,1)S(1)} %convert_element_type.179), channel_id=1, source_target_pairs={{0,252},{4,0},{8,4},{12,8},{16,12},{20,16},{24,20},{28,24},{32,28}... | collective-permute-start | bytes 147464 | tf_op jit(solution)/shard_map/ppermute | solution.py:31
  32.0 29.7 %collective-permute-start.2 = (bf16[3,4096]{1,0:T(4,128)(2,1)}, bf16[3,4096]{1,0:T(4,128)(2,1)}, u32[]{:S(2)}, u32[]{:S(2)}) collective-permute-start(bf16[3,4096]{1,0:T(4,128)(2,1)} %convert_element_type.182), channel_id=1, source_target_pairs={{0,1},{1,2},{2,3},{4,5},{5,6},{6,7},{8,9},{9,10},{10,11},{12,13},{... | collective-permute-start | bytes 73736 | tf_op jit(solution)/shard_map/ppermute | solution.py:37
  34.6 12.3 %copy-start.2 = (f32[512,2048,1,1,1]{1,0,4,3,2:T(8,128)S(1)}, f32[512,2048,1,1,1]{1,0,4,3,2:T(8,128)}, u32[]{:S(2)}) copy-start(f32[512,2048,1,1,1]{1,0,4,3,2:T(8,128)} %constant.45) | copy-start | bytes 12582916
  34.6 28.0 %collective-permute-start.3 = (bf16[3,4096]{1,0:T(4,128)(2,1)}, bf16[3,4096]{1,0:T(4,128)(2,1)}, u32[]{:S(2)}, u32[]{:S(2)}) collective-permute-start(bf16[3,4096]{1,0:T(4,128)(2,1)} %convert_element_type.185), channel_id=1, source_target_pairs={{1,0},{2,1},{3,2},{5,4},{6,5},{7,6},{9,8},{10,9},{11,10},{13,12},{... | collective-permute-start | bytes 73736 | tf_op jit(solution)/shard_map/ppermute | solution.py:37
  59.1 3.5 copy-start.10
  74.3 7.5 %copy-start.3 = (f32[512,2048,1,1,1]{1,0,4,3,2:T(8,128)S(1)}, f32[512,2048,1,1,1]{1,0,4,3,2:T(8,128)}, u32[]{:S(2)}) copy-start(f32[512,2048,1,1,1]{1,0,4,3,2:T(8,128)} %constant.45) | copy-start | bytes 12582916
  81.9 12.3 %copy-start.6 = (f32[512,384,1,1,1]{1,0,4,3,2:T(8,128)S(1)}, f32[512,384,1,1,1]{1,0,4,3,2:T(8,128)}, u32[]{:S(2)}) copy-start(f32[512,384,1,1,1]{1,0,4,3,2:T(8,128)} %constant.46) | copy-start | bytes 2359300
  104.0 24.7 %collective-permute-start.4 = (bf16[3,8192]{1,0:T(4,128)(2,1)}, bf16[3,8192]{1,0:T(4,128)(2,1)}, u32[]{:S(2)}, u32[]{:S(2)}) collective-permute-start(bf16[3,8192]{1,0:T(4,128)(2,1)} %convert_element_type.188), channel_id=1, source_target_pairs={{0,4},{4,8},{8,12},{12,16},{16,20},{20,24},{24,28},{28,32},{32,36}... | collective-permute-start | bytes 147464 | tf_op jit(solution)/shard_map/ppermute | solution.py:31
  105.6 26.5 %collective-permute-start.5 = (bf16[3,8192]{1,0:T(4,128)(2,1)}, bf16[3,8192]{1,0:T(4,128)(2,1)}, u32[]{:S(2)}, u32[]{:S(2)}) collective-permute-start(bf16[3,8192]{1,0:T(4,128)(2,1)} %convert_element_type.191), channel_id=1, source_target_pairs={{0,252},{4,0},{8,4},{12,8},{16,12},{20,16},{24,20},{28,24},{32,28}... | collective-permute-start | bytes 147464 | tf_op jit(solution)/shard_map/ppermute | solution.py:31
  111.3 11.5 %collective-permute-start.6 = (bf16[3,4096]{1,0:T(4,128)(2,1)}, bf16[3,4096]{1,0:T(4,128)(2,1)}, u32[]{:S(2)}, u32[]{:S(2)}) collective-permute-start(bf16[3,4096]{1,0:T(4,128)(2,1)} %convert_element_type.194), channel_id=1, source_target_pairs={{0,1},{1,2},{2,3},{4,5},{5,6},{6,7},{8,9},{9,10},{10,11},{12,13},{... | collective-permute-start | bytes 73736 | tf_op jit(solution)/shard_map/ppermute | solution.py:37
  113.9 12.2 %collective-permute-start.7 = (bf16[3,4096]{1,0:T(4,128)(2,1)}, bf16[3,4096]{1,0:T(4,128)(2,1)S(1)}, u32[]{:S(2)}, u32[]{:S(2)}) collective-permute-start(bf16[3,4096]{1,0:T(4,128)(2,1)} %convert_element_type.197), channel_id=1, source_target_pairs={{1,0},{2,1},{3,2},{5,4},{6,5},{7,6},{9,8},{10,9},{11,10},{13,12},{... | collective-permute-start | bytes 73736 | tf_op jit(solution)/shard_map/ppermute | solution.py:37
  138.4 7.1 %copy-start.11 = (f32[512,64,1,1]{0,1,3,2:T(8,128)S(1)}, f32[512,64,1,1]{0,1,3,2:T(8,128)}, u32[]{:S(2)}) copy-start(f32[512,64,1,1]{0,1,3,2:T(8,128)} %constant.47) | copy-start | bytes 393220
  145.4 1.1 copy-start.4
  147.9 7.1 %all-to-all-start.1 = ((bf16[2,4,32,128]{3,1,0,2:T(4,128)(2,1)}), bf16[2,4,32,128]{3,1,0,2:T(4,128)(2,1)S(1)}, u32[]{:S(2)}, u32[]{:S(2)}) async-start(bf16[2,4,32,128]{3,1,0,2:T(4,128)(2,1)} %copy.40), calls=%async_computation.1 | async-start | bytes 131072 | tf_op jit(solution)/shard_map/all_to_all | solution.py:190
  154.9 14.0 %all-to-all-start = ((bf16[2,4,32,1024]{3,1,0,2:T(4,128)(2,1)}), bf16[2,4,32,1024]{3,1,0,2:T(4,128)(2,1)S(1)}, u32[]{:S(2)}, u32[]{:S(2)}) async-start(bf16[2,4,32,1024]{3,1,0,2:T(4,128)(2,1)} %copy.37), calls=%async_computation | async-start | bytes 1048576 | tf_op jit(solution)/shard_map/all_to_all | solution.py:189
  161.7 330.0 %all-reduce.5.cloned.1.call-start = ((), (), s32[]{:S(2)}) async-start(), calls=%async_computation.2 | async-start | bytes 16515072 | tf_op jit(solution)/shard_map/psum | solution.py:204
  169.9 3.3 copy-start.8
  170.4 3.9 copy-start.7
  173.2 1.1 copy-start.12
  212.0 1.4 copy-start.5
Sparse Core Ops, SparseCore 0:
  212.1 279.4 all-reduce.4
where the time goes:
time: 513 us; the launch traced here: 505 us
  waiting for transfers between devices  273 us (53%)
  local copies, waits for them, and re-layouts  99.5 us (19%)
  matrix products  61.3 us (12%)
  starting transfers between devices  36.7 us (7%)
  other arithmetic  19 us (4%)
  between operations  14.9 us (3%)
    psum x1, waiting for transfers between devices, body(): lax.psum((grad_encode, grad_conv, grad_head), ('sim', 'grp'))  271 us
    unnamed x86, local copies, waits for them, and re-layouts  36 us
    dot_general x2, matrix products, advance(): jnp.einsum('cxyzp,pq->cxyzq', field, stencil, precision=lax.Precision.HIG...  24.5 us
    ppermute x4, starting transfers between devices, from_behind(): return lax.ppermute(block, axis, route)  14.8 us
    dot_general x2, matrix products, advance(): jnp.einsum('cxyzq,pq->cxyzp', beside - faces, select, precision=lax.Preci...  14.5 us
  transfers between devices with their start and end apart: 11, of which 3 were waited for; matrix products, arithmetic and copies ran while one was open for 12% of the time, Pallas kernels for 0%

commit v1 on v0

v1 whole, which is shorter than its diff:
```python
import jax
import jax.numpy as jnp
import ml_dtypes
import numpy as np
from jax import lax
from jax.experimental import pallas as pl
from jax.experimental.pallas import tpu as pltpu
from jax.sharding import PartitionSpec as P

NP = 8
STEPS = 2
VISCOSITY = 0.2
TIME_STEP = 0.005
PENALTY = 100.0
LOSS_WEIGHT = 64.0

MESH = pl.DeviceIdType.MESH
F32 = jnp.float32
BF16 = jnp.bfloat16

GRAD_ROWS = 2048
CONV_ROWS = 1728
ENC_ROW = 1728
HEAD_ROW = 1984
PAD_ROW = 2016


def derivative_matrix(count):
    places = np.arange(count)
    points = -np.cos(np.pi * places / (count - 1))
    weights = np.where(places % 2 == 0, 1.0, -1.0)
    weights[0] = weights[0] * 0.5
    weights[count - 1] = weights[count - 1] * 0.5
    identity = np.eye(count)
    spread = points[:, None] - points[None, :] + identity
    deriv = weights[None, :] / weights[:, None] / spread
    deriv = deriv * (1.0 - identity)
    return deriv - identity * deriv.sum(axis=1)[:, None]


def element_tables(count):
    deriv = derivative_matrix(count)
    single = np.eye(count)
    square = np.eye(count * count)
    along_x = np.kron(deriv, square)
    along_y = np.kron(single, np.kron(deriv, single))
    along_z = np.kron(square, deriv)
    laplace = along_x @ along_x + along_y @ along_y + along_z @ along_z
    grid = np.arange(count**3).reshape(count, count, count)
    final = count - 1
    chosen = np.concatenate(
        [
            grid[0].ravel(),
            grid[final].ravel(),
            grid[:, 0].ravel(),
            grid[:, final].ravel(),
            grid[:, :, 0].ravel(),
            grid[:, :, final].ravel(),
        ]
    )
    select = np.zeros((count**3, chosen.size))
    select[chosen, np.arange(chosen.size)] = 1.0
    bottom = np.zeros((count**3, 2 * count * count))
    for first in range(count):
        for middle in range(count):
            for inner in range(count):
                bottom[grid[first, middle, inner], first * count + inner] = (
                    VISCOSITY * deriv[0, middle]
                )
    diffuse = TIME_STEP * VISCOSITY * (laplace.T - PENALTY * (select @ select.T))
    half = count**3 // 2
    swapped = select.reshape(count**3, 3, 2, count * count)[:, :, ::-1].reshape(count**3, -1)
    small = lambda table: np.asarray(table, ml_dtypes.bfloat16)
    return (
        small(np.concatenate([TIME_STEP * along_x.T, diffuse], axis=1)),
        small(
            TIME_STEP
            * np.concatenate([along_y.T[:half, :half], along_z.T[:half, :half]], axis=1)
        ),
        small(select),
        small(swapped.T),
        np.asarray(bottom, np.float32),
    )


def dot(a, b):
    return lax.dot_general(a, b, (((1,), (0,)), ((), ())), preferred_element_type=F32)


def dot_rows(a, b):
    return lax.dot_general(a, b, (((0,), (0,)), ((), ())), preferred_element_type=F32)


def dot_cols(a, b):
    return lax.dot_general(a, b, (((1,), (1,)), ((), ())), preferred_element_type=F32)


def parts(value):
    high = value.astype(BF16)
    return high, (value - high.astype(F32)).astype(BF16)


def silu_grad(value):
    sigma = jax.nn.sigmoid(value)
    return sigma * (1.0 + value * (1.0 - sigma))


def lanes_low(shape):
    return lax.broadcasted_iota(jnp.int32, shape, len(shape) - 1) < 64


def remote(src, dst, send, recv, device):
    return pltpu.make_async_remote_copy(
        src_ref=src,
        dst_ref=dst,
        send_sem=send,
        recv_sem=recv,
        device_id=device,
        device_id_type=MESH,
    )


def greet(devices):
    barrier = pltpu.get_barrier_semaphore()
    for device in devices:
        pl.semaphore_signal(barrier, inc=1, device_id=device, device_id_type=MESH)
    pl.semaphore_wait(barrier, len(devices))


def flow_kernel(
    sims,
    vel_ref,
    slot_ref,
    wide_ref,
    narrow_ref,
    sel_ref,
    unsel_ref,
    bottom_ref,
    enc_ref,
    out_ref,
    h1_ref,
    z1_ref,
    snap_ref,
    target_ref,
    perm,
    field,
    partial,
    faces,
    send_x,
    send_y,
    recv_x,
    recv_y,
    send_sem,
    recv_sem,
):
    sim = lax.axis_index("sim")
    grp = lax.axis_index("grp")
    right = (lax.rem(sim + 1, sims), grp)
    left = (lax.rem(sim + sims - 1, sims), grp)
    above = (sim, lax.rem(grp + 1, 4))
    below = (sim, lax.rem(grp + 3, 4))
    greet([right, left, above, below])

    owner = lax.broadcasted_iota(jnp.int32, (256, 256), 0)
    by_slot = jnp.where(owner == slot_ref[...], 1.0, 0.0).astype(F32)
    by_place = by_slot.T
    for ix in range(2):
        for iy in range(4):
            for j in range(4):
                old = ix * 128 + iy * 32 + j * 8
                new = j * 64 + iy * 16 + ix * 8
                perm[new : new + 8] = by_place[old : old + 8]
    gather = perm[...].astype(BF16)
    for c in range(3):
        high, low = parts(vel_ref[c])
        field[0, c] = dot(gather, high) + dot(gather, low)

    for step in range(STEPS):
        now, later = step % 2, (step + 1) % 2
        for c in range(3):
            faces[c] = dot(field[now, c].astype(BF16), sel_ref[...])
            along_x = faces[c, :, 0:128].reshape(16, 2, 8, 128)
            along_y = faces[c, :, 128:256].reshape(4, 4, 16, 128)
            send_x[step, 0, c] = along_x[:, 1].reshape(128, 128).astype(BF16)
            send_x[step, 1, c] = along_x[:, 0].reshape(128, 128).astype(BF16)
            send_y[step, 0, c] = along_y[:, 3].reshape(64, 128).astype(BF16)
            send_y[step, 1, c] = along_y[:, 0].reshape(64, 128).astype(BF16)
        copies = []
        for k, (src, dst, device) in enumerate(
            [
                (send_x.at[step, 0], recv_x.at[step, 0], right),
                (send_x.at[step, 1], recv_x.at[step, 1], left),
                (send_y.at[step, 0], recv_y.at[step, 0], above),
                (send_y.at[step, 1], recv_y.at[step, 1], below),
            ]
        ):
            copy = remote(src, dst, send_sem.at[step, k], recv_sem.at[step, k], device)
            copy.start()
            copies.append(copy)
        for c in range(3):
            for row in range(0, 256, 128):
                rows = slice(row, row + 128)
                mine = field[now, c, rows].astype(BF16)
                for h in range(0, 512, 256):
                    cols = slice(h, h + 256)
                    d_x = dot(mine, wide_ref[:, h : h + 256])
                    spread = dot(mine, wide_ref[:, 512 + h : 768 + h])
                    d_y = dot(mine[:, cols], narrow_ref[:, 0:256])
                    d_z = dot(mine[:, cols], narrow_ref[:, 256:512])
                    advect = field[now, 0, rows, cols] * d_x
                    advect = advect + field[now, 1, rows, cols] * d_y
                    advect = advect + field[now, 2, rows, cols] * d_z
                    partial[c, rows, cols] = field[now, c, rows, cols] + (spread - advect)
        for copy in copies:
            copy.wait()
        for c in range(3):
            along_x = faces[c, :, 0:128].reshape(16, 2, 8, 128)
            along_y = faces[c, :, 128:256].reshape(4, 4, 16, 128)
            along_z = faces[c, :, 256:384].reshape(4, 8, 8, 128)
            from_left = recv_x[step, 0, c].astype(F32).reshape(16, 1, 8, 128)
            from_right = recv_x[step, 1, c].astype(F32).reshape(16, 1, 8, 128)
            from_below = recv_y[step, 0, c].astype(F32).reshape(4, 1, 16, 128)
            from_above = recv_y[step, 1, c].astype(F32).reshape(4, 1, 16, 128)
            from_below = jnp.where(grp > 0, from_below, 0.0)
            from_above = jnp.where(grp < 3, from_above, 0.0)
            before = jnp.concatenate([from_left, along_x[:, :1]], axis=1).reshape(256, 128)
            after = jnp.concatenate([along_x[:, 1:], from_right], axis=1).reshape(256, 128)
            low = lanes_low((256, 128))
            beside_x = jnp.where(low, after, before).astype(BF16)
            before = jnp.concatenate([from_below, along_y[:, :3]], axis=1).reshape(256, 128)
            after = jnp.concatenate([along_y[:, 1:], from_above], axis=1).reshape(256, 128)
            beside_y = jnp.where(low, after, before).astype(BF16)
            place = lax.broadcasted_iota(jnp.int32, (32, 8, 128), 1)
            flat_z = along_z.reshape(32, 8, 128)
            behind = jnp.concatenate([along_z[3:], along_z[:3]], axis=0).reshape(32, 8, 128)
            ahead = jnp.concatenate([along_z[1:], along_z[:1]], axis=0).reshape(32, 8, 128)
            before = pltpu.roll(jnp.where(place == 7, behind, flat_z), 1, 1).reshape(256, 128)
            after = pltpu.roll(jnp.where(place == 0, ahead, flat_z), 7, 1).reshape(256, 128)
            beside_z = jnp.where(low, after, before).astype(BF16)
            beside = jnp.concatenate([beside_x, beside_y, beside_z], axis=1)
            for h in range(0, 512, 256):
                cols = slice(h, h + 256)
                pull = dot(beside, unsel_ref[:, cols])
                field[later, c, :, cols] = (
                    partial[c, :, cols] + (TIME_STEP * VISCOSITY * PENALTY) * pull
                )

    final = STEPS % 2
    snap_ref[:, 0:512] = field[final, 0].astype(BF16)
    snap_ref[:, 512:1024] = field[final, 2].astype(BF16)
    z1 = dot(snap_ref[...], enc_ref[...])
    z1_ref[...] = z1
    h1_ref[...] = (z1 * jax.nn.sigmoid(z1)).astype(BF16).reshape(4, 64, 256)
    table_high, table_low = parts(bottom_ref[...])
    stress = []
    for c in (0, 2):
        high, low = parts(field[final, c])
        stress.append(dot(high, table_high) + dot(high, table_low) + dot(low, table_high))
    side = pltpu.roll(stress[1], 64, 1)
    both = jnp.where(lanes_low((256, 128)), stress[0], side).astype(BF16)
    target_ref[...] = both.reshape(4, 64, 128)
    scatter = perm[...].T.astype(BF16)
    for c in range(3):
        high, low = parts(field[final, c])
        out_ref[c] = dot(scatter, high) + dot(scatter, low)


def variants(value, width):
    place = lax.broadcasted_iota(jnp.int32, (32, 8, width), 1)
    flat = value.reshape(32, 8, width)
    along_z = {
        -1: jnp.where(place == 0, 0.0, pltpu.roll(flat, 1, 1)),
        0: flat,
        1: jnp.where(place == 7, 0.0, pltpu.roll(flat, 7, 1)),
    }
    for dz in (-1, 0, 1):
        full = along_z[dz].reshape(16, 2, 8, width)
        none = jnp.zeros((16, 1, 8, width), F32)
        yield -1, dz, jnp.concatenate([none, full[:, :1]], axis=1).reshape(256, width)
        yield 0, dz, full.reshape(256, width)
        yield 1, dz, jnp.concatenate([full[:, 1:], none], axis=1).reshape(256, width)


def train_kernel(
    h1_ref,
    target_ref,
    z1_ref,
    snap_ref,
    conv_ref,
    head_ref,
    out_ref,
    crop_h,
    crop_t,
    all_h,
    shifted,
    dz2_buf,
    all_dz2,
    shifted_low,
    shifted_high,
    taps,
    dh1_buf,
    all_dh1,
    enc_buf,
    all_enc,
    head_buf,
    all_head,
    send_sem,
    recv_sem,
):
    sim = lax.axis_index("sim")
    grp = lax.axis_index("grp")
    peers = [lax.rem(grp + d, 4) for d in (1, 2, 3)]
    greet([(sim, peer) for peer in peers])

    def block(index):
        return pl.ds(pl.multiple_of(index * 64, 64), 64)

    def exchange(kind, pairs):
        copies = []
        for d, (src, dst) in enumerate(pairs):
            copy = remote(src, dst, send_sem.at[kind, d], recv_sem.at[kind, d], (sim, peers[d]))
            copy.start()
            copies.append(copy)
        return copies

    h_copies = exchange(0, [(h1_ref.at[p], crop_h.at[grp]) for p in peers])
    t_copies = exchange(1, [(target_ref.at[p], crop_t.at[grp]) for p in peers])
    crop_h[grp] = h1_ref[grp]
    crop_t[grp] = target_ref[grp]
    all_h[:, grp] = h1_ref[...]
    whole = [(h1_ref, all_h.at[:, grp]) for p in peers]

    for k in range(9):
        shifted[k, 0:16] = jnp.zeros((16, 256), BF16)
        shifted[k, 272:288] = jnp.zeros((16, 256), BF16)
        for j in range(4):
            shifted_low[k, j, 0:16] = jnp.zeros((16, 128), BF16)
            shifted_low[k, j, 272:288] = jnp.zeros((16, 128), BF16)
            shifted_high[k, j, 0:16] = jnp.zeros((16, 128), BF16)
            shifted_high[k, j, 272:288] = jnp.zeros((16, 128), BF16)

    a_copies = exchange(2, whole)
    for copy in h_copies:
        copy.wait()
    value = crop_h[...].reshape(256, 256).astype(F32)
    for dx, dz, moved in variants(value, 256):
        shifted[3 * (dx + 1) + dz + 1, 16:272] = moved.astype(BF16)
    z2 = jnp.zeros((256, 256), F32)
    for dx in (-1, 0, 1):
        for dy in (-1, 0, 1):
            for dz in (-1, 0, 1):
                tap = 9 * (dx + 1) + 3 * (dy + 1) + dz + 1
                start = 16 * (1 + dy)
                z2 = z2 + dot(
                    shifted[3 * (dx + 1) + dz + 1, start : start + 256], conv_ref[tap]
                )
    h2 = (z2 * jax.nn.sigmoid(z2)).astype(BF16)
    output = dot(h2, head_ref[...])
    for copy in t_copies:
        copy.wait()
    target = crop_t[...].reshape(256, 128).astype(F32)
    resid = ((output - target) * (LOSS_WEIGHT / 65536.0)).astype(BF16)
    dz2 = (dot_cols(resid, head_ref[...]) * silu_grad(z2)).astype(BF16)
    dz2_buf[0] = dz2[:, 0:128]
    dz2_buf[1] = dz2[:, 128:256]
    all_dz2[grp] = dz2_buf[grp // 2]
    z_copies = exchange(3, [(dz2_buf.at[p // 2], all_dz2.at[grp]) for p in peers])
    head_buf[...] = dot_rows(h2, resid).astype(BF16).reshape(4, 64, 128)
    g_copies = exchange(4, [(head_buf.at[p], all_head.at[d]) for d, p in enumerate(peers)])

    for dx, dz, moved in variants(dz2.astype(F32), 256):
        shifted[3 * (dx + 1) + dz + 1, 16:272] = moved.astype(BF16)
    dh1 = jnp.zeros((256, 256), F32)
    for dx in (-1, 0, 1):
        for dy in (-1, 0, 1):
            for dz in (-1, 0, 1):
                tap = 9 * (dx + 1) + 3 * (dy + 1) + dz + 1
                start = 16 * (1 - dy)
                dh1 = dh1 + dot_cols(
                    shifted[3 * (1 - dx) + 1 - dz, start : start + 256], conv_ref[tap]
                )
    dh1_buf[...] = dh1.astype(BF16).reshape(4, 64, 256)
    all_dh1[grp] = dh1_buf[grp]
    d_copies = exchange(5, [(dh1_buf.at[p], all_dh1.at[grp]) for p in peers])

    for copy in z_copies:
        copy.wait()
    low = lanes_low((256, 128))
    for j in range(4):
        value = all_dz2[j].astype(F32)
        turned = pltpu.roll(value, 64, 1)
        first = lax.rem(grp, 2) == 0
        here = jnp.where(low, jnp.where(first, value, turned), jnp.where(first, turned, value))
        for dx, dz, moved in variants(here, 128):
            k = 3 * (dx + 1) + dz + 1
            shifted_low[k, j, 16:272] = jnp.where(low, moved, 0.0).astype(BF16)
            shifted_high[k, j, 16:272] = jnp.where(low, 0.0, moved).astype(BF16)
    for copy in a_copies:
        copy.wait()

    def tap_place(tap):
        dx, dy, dz = tap // 9 - 1, tap // 3 % 3 - 1, tap % 3 - 1
        return 3 * (1 - dx) + 1 - dz, 16 * (1 - dy)

    def conv_grad(pairs):
        for place, pair in enumerate(pairs):
            for j in range(4):
                k, start = tap_place(2 * pair)
                value = shifted_low[k, j, start : start + 256]
                if 2 * pair + 1 < 27:
                    k, start = tap_place(2 * pair + 1)
                    value = value + shifted_high[k, j, start : start + 256]
                taps[j * 256 : j * 256 + 256, place * 128 : place * 128 + 128] = value
        width = 128 * len(pairs)
        grad = dot_rows(taps[:, 0:width], all_h[...].reshape(1024, 256))
        first = 128 * pairs[0]
        last = min(first + width, CONV_ROWS)
        out_ref[first:last] = grad[: last - first]

    conv_grad([0, 1, 2, 3])
    conv_grad([4, 5, 6, 7])
    for copy in d_copies:
        copy.wait()
    dz1 = (all_dh1[...].reshape(256, 256).astype(F32) * silu_grad(z1_ref[...])).astype(BF16)
    for b in range(4):
        enc_buf[b] = dot_rows(dz1, snap_ref[:, b * 256 : b * 256 + 256])
    own_block = block(grp)
    for d, p in enumerate(peers):
        for b in range(4):
            all_enc[0, d, b] = enc_buf[b, block(p)].astype(BF16)
    e_copies = exchange(6, [(all_enc.at[0, d], all_enc.at[1, d]) for d in range(3)])
    conv_grad([8, 9, 10, 11])
    conv_grad([12, 13])
    for copy in e_copies + g_copies:
        copy.wait()
    for b in range(4):
        total = enc_buf[b, own_block]
        for d in range(3):
            total = total + all_enc[1, d, b].astype(F32)
        out_ref[ENC_ROW + b * 64 : ENC_ROW + b * 64 + 64] = total
    total = head_buf[grp].astype(F32)
    for d in range(3):
        total = total + all_head[d].astype(F32)
    out_ref[HEAD_ROW:PAD_ROW, 0:128] = total[0:32]
    out_ref[HEAD_ROW:PAD_ROW, 128:256] = total[32:64]
    out_ref[PAD_ROW:GRAD_ROWS] = jnp.zeros((GRAD_ROWS - PAD_ROW, 256), F32)


def reduce_kernel(
    grad_ref,
    conv_ref,
    enc_ref,
    head_ref,
    work,
    recv_x,
    work_z,
    recv_z,
    work_y,
    recv_y,
    sum_x,
    sum_z,
    result,
    send_sem,
    recv_sem,
):
    sim = lax.axis_index("sim")
    grp = lax.axis_index("grp")
    x, y, z = sim // 16, lax.rem(sim // 8, 2), lax.rem(sim, 8)
    peers_x = [lax.rem(x + d, 4) for d in range(1, 4)]
    peers_z = [lax.rem(z + d, 8) for d in range(1, 8)]
    dev_x = [(p * 16 + y * 8 + z, grp) for p in peers_x]
    dev_z = [(x * 16 + y * 8 + p, grp) for p in peers_z]
    dev_y = (x * 16 + (1 - y) * 8 + z, grp)
    greet(dev_x + dev_z + [dev_y])

    def rows(index, count):
        return pl.ds(pl.multiple_of(index * count, count), count)

    def start(base, triples):
        copies = []
        for d, (src, dst, device) in enumerate(triples):
            copy = remote(src, dst, send_sem.at[base + d], recv_sem.at[base + d], device)
            copy.start()
            copies.append(copy)
        return copies

    def finish(copies):
        for copy in copies:
            copy.wait()

    work[...] = grad_ref[...].astype(BF16)
    copies = start(
        0, [(work.at[rows(peers_x[d], 512)], recv_x.at[d], dev_x[d]) for d in range(3)]
    )
    finish(copies)
    total = grad_ref[rows(x, 512)]
    for d in range(3):
        total = total + recv_x[d].astype(F32)
    sum_x[...] = total
    work_z[...] = total.astype(BF16)
    copies = start(
        3, [(work_z.at[rows(peers_z[d], 64)], recv_z.at[d], dev_z[d]) for d in range(7)]
    )
    finish(copies)
    total = sum_x[rows(z, 64)]
    for d in range(7):
        total = total + recv_z[d].astype(F32)
    sum_z[...] = total
    work_y[...] = total.astype(BF16)
    finish(start(10, [(work_y.at[rows(1 - y, 32)], recv_y, dev_y)]))
    total = sum_z[rows(y, 32)] + recv_y[...].astype(F32)
    base = x * 512 + z * 64
    mine = pl.ds(pl.multiple_of(base + y * 32, 32), 32)
    result[mine] = total.astype(BF16)
    finish(start(11, [(result.at[mine], result.at[mine], dev_y)]))
    mine = pl.ds(pl.multiple_of(base, 64), 64)
    finish(start(12, [(result.at[mine], result.at[mine], dev_z[d]) for d in range(7)]))
    mine = rows(x, 512)
    finish(start(19, [(result.at[mine], result.at[mine], dev_x[d]) for d in range(3)]))
    conv_ref[...] = result[0:CONV_ROWS].astype(F32)
    for b in range(4):
        enc_ref[:, b * 256 : b * 256 + 256] = result[
            ENC_ROW + b * 64 : ENC_ROW + b * 64 + 64
        ].astype(F32)
    head_ref[0:32] = result[HEAD_ROW:PAD_ROW, 0:128].astype(F32)
    head_ref[32:64] = result[HEAD_ROW:PAD_ROW, 128:256].astype(F32)


VM = pl.BlockSpec(memory_space=pltpu.VMEM)


def shaped(shape, dtype):
    return jax.ShapeDtypeStruct(shape, dtype)


def reduced(grads):
    dma = pltpu.SemaphoreType.DMA
    return pl.pallas_call(
        reduce_kernel,
        out_shape=(
            shaped((CONV_ROWS, 256), F32),
            shaped((64, 1024), F32),
            shaped((64, 128), F32),
        ),
        in_specs=[VM],
        out_specs=(VM, VM, VM),
        scratch_shapes=[
            pltpu.VMEM((GRAD_ROWS, 256), BF16),
            pltpu.VMEM((3, 512, 256), BF16),
            pltpu.VMEM((512, 256), BF16),
            pltpu.VMEM((7, 64, 256), BF16),
            pltpu.VMEM((64, 256), BF16),
            pltpu.VMEM((32, 256), BF16),
            pltpu.VMEM((512, 256), F32),
            pltpu.VMEM((64, 256), F32),
            pltpu.VMEM((GRAD_ROWS, 256), BF16),
            dma((22,)),
            dma((22,)),
        ],
        compiler_params=pltpu.CompilerParams(
            collective_id=2, has_side_effects=True, vmem_limit_bytes=32 * 2**20
        ),
    )(grads)


def body(velocity, slot_of, w_encode, w_conv, w_head):
    wide, narrow, select, unselect, bottom = element_tables(NP)
    dma = pltpu.SemaphoreType.DMA
    flow = pl.pallas_call(
        lambda *refs: flow_kernel(lax.axis_size("sim"), *refs),
        name="flow",
        out_shape=(
            shaped((3, 256, 512), F32),
            shaped((4, 64, 256), BF16),
            shaped((256, 256), F32),
            shaped((256, 1024), BF16),
            shaped((4, 64, 128), BF16),
        ),
        in_specs=[VM] * 8,
        out_specs=(VM,) * 5,
        scratch_shapes=[
            pltpu.VMEM((256, 256), F32),
            pltpu.VMEM((2, 3, 256, 512), F32),
            pltpu.VMEM((3, 256, 512), F32),
            pltpu.VMEM((3, 256, 384), F32),
            pltpu.VMEM((STEPS, 2, 3, 128, 128), BF16),
            pltpu.VMEM((STEPS, 2, 3, 64, 128), BF16),
            pltpu.VMEM((STEPS, 2, 3, 128, 128), BF16),
            pltpu.VMEM((STEPS, 2, 3, 64, 128), BF16),
            dma((STEPS, 4)),
            dma((STEPS, 4)),
        ],
        compiler_params=pltpu.CompilerParams(
            collective_id=0, has_side_effects=True, vmem_limit_bytes=48 * 2**20
        ),
    )
    velocity_next, h1, z1, snapshot, target = flow(
        velocity[0, 0], slot_of[0], wide, narrow, select, unselect, bottom, w_encode
    )
    train = pl.pallas_call(
        train_kernel,
        name="train",
        out_shape=shaped((GRAD_ROWS, 256), F32),
        in_specs=[VM] * 6,
        out_specs=VM,
        scratch_shapes=[
            pltpu.VMEM((4, 64, 256), BF16),
            pltpu.VMEM((4, 64, 128), BF16),
            pltpu.VMEM((4, 4, 64, 256), BF16),
            pltpu.VMEM((9, 288, 256), BF16),
            pltpu.VMEM((2, 256, 128), BF16),
            pltpu.VMEM((4, 256, 128), BF16),
            pltpu.VMEM((9, 4, 288, 128), BF16),
            pltpu.VMEM((9, 4, 288, 128), BF16),
            pltpu.VMEM((1024, 512), BF16),
            pltpu.VMEM((4, 64, 256), BF16),
            pltpu.VMEM((4, 64, 256), BF16),
            pltpu.VMEM((4, 256, 256), F32),
            pltpu.VMEM((2, 3, 4, 64, 256), BF16),
            pltpu.VMEM((4, 64, 128), BF16),
            pltpu.VMEM((3, 64, 128), BF16),
            dma((7, 3)),
            dma((7, 3)),
        ],
        compiler_params=pltpu.CompilerParams(
            collective_id=1, has_side_effects=True, vmem_limit_bytes=48 * 2**20
        ),
    )
    grads = train(h1, target, z1, snapshot, w_conv, w_head)
    conv, encode, head = reduced(grads)
    return (
        velocity_next[None, None],
        encode.T,
        conv.reshape(27, 64, 256).transpose(0, 2, 1),
        head,
    )


def solution(mesh):
    placed = (P("sim", "grp", None, None, None), P("sim", "grp", None), P(), P(), P())
    return jax.shard_map(
        body,
        mesh=mesh,
        in_specs=placed,
        out_specs=(
            P("sim", "grp", None, None, None),
            P(None, "grp"),
            P(None, None, "grp"),
            P("grp", None),
        ),
        check_vma=False,
    )
```

time: 513 us -> 114 us (0.22)
  the two profiles are of different devices: /device:TPU:24 before, /device:TPU:64 now
where the time goes in v1:
time: 114 us
  Pallas kernels  102 us (89%)
  local copies, waits for them, and re-layouts  10.5 us (9%)
    pallas_call x1, Pallas kernels, reduced(): pl.pallas_call(reduce_kernel, out_shape=(shaped((CONV_ROWS, 256), F32), s...  55.4 us
    pallas_call x1, Pallas kernels, body(): grads = train(h1, target, z1, snapshot, w_conv, w_head)  27.2 us
    pallas_call x1, Pallas kernels, body(): flow(velocity[0, 0], slot_of[0], wide, narrow, select, unselect, bottom,...  19.8 us
    unnamed x20, local copies, waits for them, and re-layouts  10.5 us

profile of v1, /device:TPU:64, one launch (start us, length us, event | category | flops | bytes accessed | tf_op | source)
XLA Modules:
  0.0 113.6 jit_solution(13064371496435354324)
XLA Ops:
  0.6 0.0 copy-start
  0.6 1.2 %copy-done = bf16[512,1024]{1,0:T(8,128)(2,1)S(1)} copy-done((bf16[512,1024]{1,0:T(8,128)(2,1)S(1)}, bf16[512,1024]{1,0:T(8,128)(2,1)}, u32[]{:S(2)}) %copy-start) | copy-done | bytes 1048600
  1.9 0.0 copy-start.1
  1.9 1.0 copy-done.1
  2.9 0.0 copy-start.2
  2.9 1.0 copy-done.2
  3.9 0.0 copy-start.3
  3.9 1.0 copy-done.3
  4.9 0.0 copy-start.4
  4.9 0.9 copy-done.4
  5.8 0.0 copy-start.5
  5.8 0.9 copy-done.5
  6.8 0.0 copy-start.7
  6.8 0.7 copy-done.7
  7.5 0.0 copy-start.6
  7.5 19.8 %flow.1 = (f32[3,256,512]{2,1,0:T(8,128)S(1)}, bf16[4,64,256]{2,1,0:T(8,128)(2,1)S(1)}, f32[256,256]{1,0:T(8,128)S(1)}, bf16[256,1024]{1,0:T(8,128)(2,1)S(1)}, bf16[4,64,128]{2,1,0:T(8,128)(2,1)S(1)}) custom-call(f32[3,256,512]{2,1,0:T(8,128)} %bitcast.11, s32[1,256]{1,0:T(1,128)S(1)} %bitcast.10, bf16[512,1024]{1,0:T(8,128)(2,1)S(1)} %copy-done, ...), custom_call_target="tpu_custom_call" | custom-call | tf_op jit(solution)/shard_map/flow/pallas_call | solution.py:597
  27.3 0.0 copy-done.6
  27.3 27.2 %train.1.grad_ref = f32[2048,256]{1,0:T(8,128)S(1)} custom-call(bf16[4,64,256]{2,1,0:T(8,128)(2,1)S(1)} %get-tuple-element.13.h1_ref, bf16[4,64,128]{2,1,0:T(8,128)(2,1)S(1)} %get-tuple-element.14.target_ref, f32[256,256]{1,0:T(8,128)S(1)} %get-tuple-element.15.z1_ref, bf16[256,1024]{1,0:T(8,128)(2,1)S(1)} %get-tuple-element.16.snap_ref, ...), custom_call_target="tpu_custom_call" | custom-call | tf_op jit(solution)/shard_map/train/pallas_call | solution.py:629
  54.5 55.4 %shard_map.129 = (f32[1728,256]{1,0:T(8,128)S(1)}, f32[64,1024]{1,0:T(8,128)S(1)}, f32[64,128]{1,0:T(8,128)S(1)}) custom-call(f32[2048,256]{1,0:T(8,128)S(1)} %train.1.grad_ref), custom_call_target="tpu_custom_call" | custom-call | tf_op jit(solution)/shard_map/pallas_call | solution.py:538
  109.9 1.1 %copy.18 = f32[1,1,3,256,512]{4,3,2,1,0:T(8,128)} copy(f32[1,1,3,256,512]{4,3,2,1,0:T(8,128)S(1)} %bitcast.8) | data formatting | bytes 3145728
  111.1 0.7 copy.19
  111.8 1.2 %copy.20 = f32[27,256,64]{1,2,0:T(8,128)} copy(f32[27,256,64]{1,2,0:T(8,128)S(1)} %bitcast.7) | data formatting | bytes 3538944
  113.0 0.6 copy.21
Async XLA Ops:
  0.6 1.2 %copy-start = (bf16[512,1024]{1,0:T(8,128)(2,1)S(1)}, bf16[512,1024]{1,0:T(8,128)(2,1)}, u32[]{:S(2)}) copy-start(bf16[512,1024]{1,0:T(8,128)(2,1)} %constant.10.clone.refs_2_) | copy-start | bytes 3145732
  1.9 1.0 copy-start.1
  2.9 1.0 copy-start.2
  3.9 1.0 copy-start.3
  4.9 0.9 copy-start.4
  5.8 0.9 copy-start.5
  6.8 0.7 copy-start.7
  7.5 19.8 %copy-start.6 = (bf16[256,128]{1,0:T(8,128)(2,1)S(1)}, bf16[256,128]{1,0:T(8,128)(2,1)}, u32[]{:S(2)}) copy-start(bf16[256,128]{1,0:T(8,128)(2,1)} %head_ref.1) | copy-start | bytes 196612

commit v2 on v1

--- a/solution.py
+++ b/solution.py
@@ -18,11 +18,8 @@
 F32 = jnp.float32
 BF16 = jnp.bfloat16
 
-GRAD_ROWS = 2048
 CONV_ROWS = 1728
-ENC_ROW = 1728
-HEAD_ROW = 1984
-PAD_ROW = 2016
+PARTS = 4
 
 
 def derivative_matrix(count):
@@ -127,8 +124,36 @@
     pl.semaphore_wait(barrier, len(devices))
 
 
-def flow_kernel(
+def variants(value, width):
+    place = lax.broadcasted_iota(jnp.int32, (32, 8, width), 1)
+    flat = value.reshape(32, 8, width)
+    along_z = {
+        -1: jnp.where(place == 0, 0.0, pltpu.roll(flat, 1, 1)),
+        0: flat,
+        1: jnp.where(place == 7, 0.0, pltpu.roll(flat, 7, 1)),
+    }
+    for dz in (-1, 0, 1):
+        full = along_z[dz].reshape(16, 2, 8, width)
+        none = jnp.zeros((16, 1, 8, width), F32)
+        yield -1, dz, jnp.concatenate([none, full[:, :1]], axis=1).reshape(256, width)
+        yield 0, dz, full.reshape(256, width)
+        yield 1, dz, jnp.concatenate([full[:, 1:], none], axis=1).reshape(256, width)
+
+
+def step_kernel(
     sims,
+    vel_hbm,
+    slot_hbm,
+    wide_hbm,
+    narrow_hbm,
+    sel_hbm,
+    unsel_hbm,
+    bottom_hbm,
+    enc_hbm,
+    conv_hbm,
+    head_hbm,
+    out_ref,
+    result,
     vel_ref,
     slot_ref,
     wide_ref,
@@ -137,11 +162,9 @@
     unsel_ref,
     bottom_ref,
     enc_ref,
-    out_ref,
-    h1_ref,
-    z1_ref,
-    snap_ref,
-    target_ref,
+    conv_ref,
+    head_ref,
+    load_sem,
     perm,
     field,
     partial,
@@ -150,17 +173,72 @@
     send_y,
     recv_x,
     recv_y,
-    send_sem,
-    recv_sem,
+    halo_send,
+    halo_recv,
+    h1_ref,
+    z1_ref,
+    snap_ref,
+    target_ref,
+    crop_h,
+    crop_t,
+    all_h,
+    shifted,
+    dz2_buf,
+    all_dz2,
+    shifted_low,
+    shifted_high,
+    taps,
+    dh1_buf,
+    all_dh1,
+    enc_buf,
+    enc_out,
+    all_enc,
+    head_buf,
+    all_head,
+    grp_send,
+    grp_recv,
+    work,
+    recv_first,
+    work_second,
+    recv_second,
+    sum_send,
+    sum_recv,
 ):
     sim = lax.axis_index("sim")
     grp = lax.axis_index("grp")
+
+    loads = []
+    for k, (src, dst) in enumerate(
+        [
+            (slot_hbm, slot_ref),
+            (vel_hbm, vel_ref),
+            (sel_hbm, sel_ref),
+            (wide_hbm, wide_ref),
+            (narrow_hbm, narrow_ref),
+            (unsel_hbm, unsel_ref),
+            (enc_hbm, enc_ref),
+            (bottom_hbm, bottom_ref),
+            (conv_hbm, conv_ref),
+            (head_hbm, head_ref),
+        ]
+    ):
+        copy = pltpu.make_async_copy(src, dst, load_sem.at[k])
+        copy.start()
+        loads.append(copy)
+
     right = (lax.rem(sim + 1, sims), grp)
     left = (lax.rem(sim + sims - 1, sims), grp)
     above = (sim, lax.rem(grp + 1, 4))
     below = (sim, lax.rem(grp + 3, 4))
-    greet([right, left, above, below])
-
+    peers = [lax.rem(grp + d, 4) for d in (1, 2, 3)]
+    plane, depth = sim // 8, lax.rem(sim, 8)
+    peers_plane = [lax.rem(plane + d, 8) for d in range(1, 8)]
+    peers_depth = [lax.rem(depth + d, 8) for d in range(1, 8)]
+    dev_plane = [(p * 8 + depth, grp) for p in peers_plane]
+    dev_depth = [(plane * 8 + p, grp) for p in peers_depth]
+    greet([left, right] + [(sim, peer) for peer in peers] + dev_plane + dev_depth)
+
+    loads[0].wait()
     owner = lax.broadcasted_iota(jnp.int32, (256, 256), 0)
     by_slot = jnp.where(owner == slot_ref[...], 1.0, 0.0).astype(F32)
     by_place = by_slot.T
@@ -171,9 +249,12 @@
                 new = j * 64 + iy * 16 + ix * 8
                 perm[new : new + 8] = by_place[old : old + 8]
     gather = perm[...].astype(BF16)
+    loads[1].wait()
     for c in range(3):
         high, low = parts(vel_ref[c])
         field[0, c] = dot(gather, high) + dot(gather, low)
+    for copy in loads[2:6]:
+        copy.wait()
 
     for step in range(STEPS):
         now, later = step % 2, (step + 1) % 2
@@ -194,7 +275,7 @@
                 (send_y.at[step, 1], recv_y.at[step, 1], below),
             ]
         ):
-            copy = remote(src, dst, send_sem.at[step, k], recv_sem.at[step, k], device)
+            copy = remote(src, dst, halo_send.at[step, k], halo_recv.at[step, k], device)
             copy.start()
             copies.append(copy)
         for c in range(3):
@@ -248,9 +329,24 @@
     final = STEPS % 2
     snap_ref[:, 0:512] = field[final, 0].astype(BF16)
     snap_ref[:, 512:1024] = field[final, 2].astype(BF16)
+    for copy in loads[6:]:
+        copy.wait()
+
+    def block(index):
+        return pl.ds(pl.multiple_of(index * 64, 64), 64)
+
+    def exchange(kind, pairs):
+        copies = []
+        for d, (src, dst) in enumerate(pairs):
+            copy = remote(src, dst, grp_send.at[kind, d], grp_recv.at[kind, d], (sim, peers[d]))
+            copy.start()
+            copies.append(copy)
+        return copies
+
     z1 = dot(snap_ref[...], enc_ref[...])
     z1_ref[...] = z1
     h1_ref[...] = (z1 * jax.nn.sigmoid(z1)).astype(BF16).reshape(4, 64, 256)
+    h_copies = exchange(0, [(h1_ref.at[p], crop_h.at[grp]) for p in peers])
     table_high, table_low = parts(bottom_ref[...])
     stress = []
     for c in (0, 2):
@@ -259,77 +355,11 @@
     side = pltpu.roll(stress[1], 64, 1)
     both = jnp.where(lanes_low((256, 128)), stress[0], side).astype(BF16)
     target_ref[...] = both.reshape(4, 64, 128)
-    scatter = perm[...].T.astype(BF16)
-    for c in range(3):
-        high, low = parts(field[final, c])
-        out_ref[c] = dot(scatter, high) + dot(scatter, low)
-
-
-def variants(value, width):
-    place = lax.broadcasted_iota(jnp.int32, (32, 8, width), 1)
-    flat = value.reshape(32, 8, width)
-    along_z = {
-        -1: jnp.where(place == 0, 0.0, pltpu.roll(flat, 1, 1)),
-        0: flat,
-        1: jnp.where(place == 7, 0.0, pltpu.roll(flat, 7, 1)),
-    }
-    for dz in (-1, 0, 1):
-        full = along_z[dz].reshape(16, 2, 8, width)
-        none = jnp.zeros((16, 1, 8, width), F32)
-        yield -1, dz, jnp.concatenate([none, full[:, :1]], axis=1).reshape(256, width)
-        yield 0, dz, full.reshape(256, width)
-        yield 1, dz, jnp.concatenate([full[:, 1:], none], axis=1).reshape(256, width)
-
-
-def train_kernel(
-    h1_ref,
-    target_ref,
-    z1_ref,
-    snap_ref,
-    conv_ref,
-    head_ref,
-    out_ref,
-    crop_h,
-    crop_t,
-    all_h,
-    shifted,
-    dz2_buf,
-    all_dz2,
-    shifted_low,
-    shifted_high,
-    taps,
-    dh1_buf,
-    all_dh1,
-    enc_buf,
-    all_enc,
-    head_buf,
-    all_head,
-    send_sem,
-    recv_sem,
-):
-    sim = lax.axis_index("sim")
-    grp = lax.axis_index("grp")
-    peers = [lax.rem(grp + d, 4) for d in (1, 2, 3)]
-    greet([(sim, peer) for peer in peers])
-
-    def block(index):
-        return pl.ds(pl.multiple_of(index * 64, 64), 64)
-
-    def exchange(kind, pairs):
-        copies = []
-        for d, (src, dst) in enumerate(pairs):
-            copy = remote(src, dst, send_sem.at[kind, d], recv_sem.at[kind, d], (sim, peers[d]))
-            copy.start()
-            copies.append(copy)
-        return copies
-
-    h_copies = exchange(0, [(h1_ref.at[p], crop_h.at[grp]) for p in peers])
     t_copies = exchange(1, [(target_ref.at[p], crop_t.at[grp]) for p in peers])
+    a_copies = exchange(2, [(h1_ref, all_h.at[:, grp]) for p in peers])
     crop_h[grp] = h1_ref[grp]
     crop_t[grp] = target_ref[grp]
     all_h[:, grp] = h1_ref[...]
-    whole = [(h1_ref, all_h.at[:, grp]) for p in peers]
-
     for k in range(9):
         shifted[k, 0:16] = jnp.zeros((16, 256), BF16)
         shifted[k, 272:288] = jnp.zeros((16, 256), BF16)
@@ -338,8 +368,11 @@
             shifted_low[k, j, 272:288] = jnp.zeros((16, 128), BF16)
             shifted_high[k, j, 0:16] = jnp.zeros((16, 128), BF16)
             shifted_high[k, j, 272:288] = jnp.zeros((16, 128), BF16)
-
-    a_copies = exchange(2, whole)
+    scatter = perm[...].T.astype(BF16)
+    for c in range(3):
+        high, low = parts(field[final, c])
+        out_ref[c] = dot(scatter, high) + dot(scatter, low)
+
     for copy in h_copies:
         copy.wait()
     value = crop_h[...].reshape(256, 256).astype(F32)
@@ -402,7 +435,8 @@
         dx, dy, dz = tap // 9 - 1, tap // 3 % 3 - 1, tap % 3 - 1
         return 3 * (1 - dx) + 1 - dz, 16 * (1 - dy)
 
-    def conv_grad(pairs):
+    def conv_grad(part):
+        pairs = range(4 * part, min(4 * part + 4, 14))
         for place, pair in enumerate(pairs):
             for j in range(4):
                 k, start = tap_place(2 * pair)
@@ -412,222 +446,212 @@
                     value = value + shifted_high[k, j, start : start + 256]
                 taps[j * 256 : j * 256 + 256, place * 128 : place * 128 + 128] = value
         width = 128 * len(pairs)
-        grad = dot_rows(taps[:, 0:width], all_h[...].reshape(1024, 256))
-        first = 128 * pairs[0]
-        last = min(first + width, CONV_ROWS)
-        out_ref[first:last] = grad[: last - first]
-
-    conv_grad([0, 1, 2, 3])
-    conv_grad([4, 5, 6, 7])
+        grad = dot_rows(taps[:, 0:width], all_h[...].reshape(1024, 256)).astype(BF16)
+        count = min(512, CONV_ROWS - 512 * part)
+        for half in range(2):
+            work[part, 32 * half : 32 * half + count // 16] = grad[
+                0:count, 128 * half : 128 * half + 128
+            ].reshape(count // 16, 16, 128)
+
+    def spread(part, phase, triples):
+        copies = []
+        for d, (src, dst, device) in enumerate(triples):
+            copy = remote(
+                src, dst, sum_send.at[part, phase, d], sum_recv.at[part, phase, d], device
+            )
+            copy.start()
+            copies.append(copy)
+        return copies
+
+    depth_way = (depth, peers_depth, dev_depth)
+    plane_way = (plane, peers_plane, dev_plane)
+    ways = [(depth_way, plane_way)] + [(plane_way, depth_way)] * (PARTS - 1)
+    flying = {}
+
+    def eight(index):
+        return pl.ds(pl.multiple_of(index * 8, 8), 8)
+
+    def advance(part, phase):
+        (a, first, dev_first), (b, second, dev_second) = ways[part]
+        if phase > 0:
+            for copy in flying[part]:
+                copy.wait()
+        if phase == 0:
+            triples = [
+                (work.at[part, eight(first[d])], recv_first.at[part, d], dev_first[d])
+                for d in range(7)
+            ]
+        if phase == 1:
+            total = work[part, eight(a)].astype(F32)
+            for d in range(7):
+                total = total + recv_first[part, d].astype(F32)
+            work_second[part] = total.astype(BF16)
+            triples = [
+                (work_second.at[part, second[d]], recv_second.at[part, d], dev_second[d])
+                for d in range(7)
+            ]
+        if phase == 2:
+            total = work_second[part, b].astype(F32)
+            for d in range(7):
+                total = total + recv_second[part, d].astype(F32)
+            mine = a * 8 + b
+            result[part, mine] = total.astype(BF16)
+            triples = [
+                (result.at[part, mine], result.at[part, mine], dev_second[d]) for d in range(7)
+            ]
+        if phase == 3:
+            mine = eight(a)
+            triples = [
+                (result.at[part, mine], result.at[part, mine], dev_first[d]) for d in range(7)
+            ]
+        if phase < 4:
+            flying[part] = spread(part, phase, triples)
+
+    conv_grad(0)
+    advance(0, 0)
     for copy in d_copies:
         copy.wait()
     dz1 = (all_dh1[...].reshape(256, 256).astype(F32) * silu_grad(z1_ref[...])).astype(BF16)
     for b in range(4):
         enc_buf[b] = dot_rows(dz1, snap_ref[:, b * 256 : b * 256 + 256])
-    own_block = block(grp)
     for d, p in enumerate(peers):
         for b in range(4):
-            all_enc[0, d, b] = enc_buf[b, block(p)].astype(BF16)
-    e_copies = exchange(6, [(all_enc.at[0, d], all_enc.at[1, d]) for d in range(3)])
-    conv_grad([8, 9, 10, 11])
-    conv_grad([12, 13])
+            enc_out[d, b] = enc_buf[b, block(p)].astype(BF16)
+    e_copies = exchange(6, [(enc_out.at[d], all_enc.at[d]) for d in range(3)])
+    conv_grad(1)
+    advance(1, 0)
+    conv_grad(2)
+    advance(2, 0)
+    advance(0, 1)
+    conv_grad(3)
     for copy in e_copies + g_copies:
         copy.wait()
     for b in range(4):
-        total = enc_buf[b, own_block]
+        total = enc_buf[b, block(grp)]
         for d in range(3):
-            total = total + all_enc[1, d, b].astype(F32)
-        out_ref[ENC_ROW + b * 64 : ENC_ROW + b * 64 + 64] = total
+            total = total + all_enc[d, b].astype(F32)
+        total = total.astype(BF16)
+        for half in range(2):
+            place = 32 * half + 12 + 4 * b
+            work[3, place : place + 4] = total[:, 128 * half : 128 * half + 128].reshape(4, 16, 128)
     total = head_buf[grp].astype(F32)
     for d in range(3):
         total = total + all_head[d].astype(F32)
-    out_ref[HEAD_ROW:PAD_ROW, 0:128] = total[0:32]
-    out_ref[HEAD_ROW:PAD_ROW, 128:256] = total[32:64]
-    out_ref[PAD_ROW:GRAD_ROWS] = jnp.zeros((GRAD_ROWS - PAD_ROW, 256), F32)
-
-
-def reduce_kernel(
-    grad_ref,
-    conv_ref,
-    enc_ref,
-    head_ref,
-    work,
-    recv_x,
-    work_z,
-    recv_z,
-    work_y,
-    recv_y,
-    sum_x,
-    sum_z,
-    result,
-    send_sem,
-    recv_sem,
-):
-    sim = lax.axis_index("sim")
-    grp = lax.axis_index("grp")
-    x, y, z = sim // 16, lax.rem(sim // 8, 2), lax.rem(sim, 8)
-    peers_x = [lax.rem(x + d, 4) for d in range(1, 4)]
-    peers_z = [lax.rem(z + d, 8) for d in range(1, 8)]
-    dev_x = [(p * 16 + y * 8 + z, grp) for p in peers_x]
-    dev_z = [(x * 16 + y * 8 + p, grp) for p in peers_z]
-    dev_y = (x * 16 + (1 - y) * 8 + z, grp)
-    greet(dev_x + dev_z + [dev_y])
-
-    def rows(index, count):
-        return pl.ds(pl.multiple_of(index * count, count), count)
-
-    def start(base, triples):
-        copies = []
-        for d, (src, dst, device) in enumerate(triples):
-            copy = remote(src, dst, send_sem.at[base + d], recv_sem.at[base + d], device)
-            copy.start()
-            copies.append(copy)
-        return copies
-
-    def finish(copies):
-        for copy in copies:
-            copy.wait()
-
-    work[...] = grad_ref[...].astype(BF16)
-    copies = start(
-        0, [(work.at[rows(peers_x[d], 512)], recv_x.at[d], dev_x[d]) for d in range(3)]
-    )
-    finish(copies)
-    total = grad_ref[rows(x, 512)]
-    for d in range(3):
-        total = total + recv_x[d].astype(F32)
-    sum_x[...] = total
-    work_z[...] = total.astype(BF16)
-    copies = start(
-        3, [(work_z.at[rows(peers_z[d], 64)], recv_z.at[d], dev_z[d]) for d in range(7)]
-    )
-    finish(copies)
-    total = sum_x[rows(z, 64)]
-    for d in range(7):
-        total = total + recv_z[d].astype(F32)
-    sum_z[...] = total
-    work_y[...] = total.astype(BF16)
-    finish(start(10, [(work_y.at[rows(1 - y, 32)], recv_y, dev_y)]))
-    total = sum_z[rows(y, 32)] + recv_y[...].astype(F32)
-    base = x * 512 + z * 64
-    mine = pl.ds(pl.multiple_of(base + y * 32, 32), 32)
-    result[mine] = total.astype(BF16)
-    finish(start(11, [(result.at[mine], result.at[mine], dev_y)]))
-    mine = pl.ds(pl.multiple_of(base, 64), 64)
-    finish(start(12, [(result.at[mine], result.at[mine], dev_z[d]) for d in range(7)]))
-    mine = rows(x, 512)
-    finish(start(19, [(result.at[mine], result.at[mine], dev_x[d]) for d in range(3)]))
-    conv_ref[...] = result[0:CONV_ROWS].astype(F32)
-    for b in range(4):
-        enc_ref[:, b * 256 : b * 256 + 256] = result[
-            ENC_ROW + b * 64 : ENC_ROW + b * 64 + 64
-        ].astype(F32)
-    head_ref[0:32] = result[HEAD_ROW:PAD_ROW, 0:128].astype(F32)
-    head_ref[32:64] = result[HEAD_ROW:PAD_ROW, 128:256].astype(F32)
+    total = total.astype(BF16).reshape(4, 16, 128)
+    for half in range(2):
+        work[3, 32 * half + 28 : 32 * half + 30] = total[2 * half : 2 * half + 2]
+        work[3, 32 * half + 30 : 32 * half + 32] = jnp.zeros((2, 16, 128), BF16)
+    advance(3, 0)
+    for part, phase in ORDER:
+        advance(part, phase)
+
+
+ORDER = [
+    (1, 1), (0, 2), (2, 1), (3, 1), (1, 2), (0, 3), (2, 2), (3, 2),
+    (1, 3), (2, 3), (3, 3), (0, 4), (1, 4), (2, 4), (3, 4),
+]
+
+
+def finish_kernel(result, vel_in, conv_ref, enc_ref, head_ref, vel_ref):
+    vel_ref[...] = vel_in[...]
+    for part in range(PARTS):
+        count = min(512, CONV_ROWS - 512 * part)
+        for half in range(2):
+            lanes = slice(128 * half, 128 * half + 128)
+            value = result[part, 32 * half : 32 * half + count // 16].astype(F32)
+            conv_ref[512 * part : 512 * part + count, lanes] = value.reshape(count, 128)
+    for half in range(2):
+        for b in range(4):
+            place = 32 * half + 12 + 4 * b
+            value = result[3, place : place + 4].astype(F32).reshape(64, 128)
+            enc_ref[:, 256 * b + 128 * half : 256 * b + 128 * half + 128] = value
+        value = result[3, 32 * half + 28 : 32 * half + 30].astype(F32).reshape(32, 128)
+        head_ref[32 * half : 32 * half + 32] = value
 
 
 VM = pl.BlockSpec(memory_space=pltpu.VMEM)
+HB = pl.BlockSpec(memory_space=pltpu.HBM)
 
 
 def shaped(shape, dtype):
     return jax.ShapeDtypeStruct(shape, dtype)
 
 
-def reduced(grads):
+def body(velocity, slot_of, w_encode, w_conv, w_head):
+    tables = element_tables(NP)
     dma = pltpu.SemaphoreType.DMA
-    return pl.pallas_call(
-        reduce_kernel,
+    vm = pltpu.VMEM
+    inputs = (velocity[0, 0], slot_of[0], *tables, w_encode, w_conv, w_head)
+    velocity_next, result = pl.pallas_call(
+        lambda *refs: step_kernel(lax.axis_size("sim"), *refs),
+        name="step",
+        out_shape=(shaped((3, 256, 512), F32), shaped((PARTS, 64, 16, 128), BF16)),
+        in_specs=[HB] * len(inputs),
+        out_specs=(VM, VM),
+        scratch_shapes=[
+            vm((3, 256, 512), F32),
+            vm((1, 256), jnp.int32),
+            *[vm(table.shape, table.dtype) for table in tables],
+            vm((1024, 256), BF16),
+            vm((27, 256, 256), BF16),
+            vm((256, 128), BF16),
+            dma((len(inputs),)),
+            vm((256, 256), F32),
+            vm((2, 3, 256, 512), F32),
+            vm((3, 256, 512), F32),
+            vm((3, 256, 384), F32),
+            vm((STEPS, 2, 3, 128, 128), BF16),
+            vm((STEPS, 2, 3, 64, 128), BF16),
+            vm((STEPS, 2, 3, 128, 128), BF16),
+            vm((STEPS, 2, 3, 64, 128), BF16),
+            dma((STEPS, 4)),
+            dma((STEPS, 4)),
+            vm((4, 64, 256), BF16),
+            vm((256, 256), F32),
+            vm((256, 1024), BF16),
+            vm((4, 64, 128), BF16),
+            vm((4, 64, 256), BF16),
+            vm((4, 64, 128), BF16),
+            vm((4, 4, 64, 256), BF16),
+            vm((9, 288, 256), BF16),
+            vm((2, 256, 128), BF16),
+            vm((4, 256, 128), BF16),
+            vm((9, 4, 288, 128), BF16),
+            vm((9, 4, 288, 128), BF16),
+            vm((1024, 512), BF16),
+            vm((4, 64, 256), BF16),
+            vm((4, 64, 256), BF16),
+            vm((4, 256, 256), F32),
+            vm((3, 4, 64, 256), BF16),
+            vm((3, 4, 64, 256), BF16),
+            vm((4, 64, 128), BF16),
+            vm((3, 64, 128), BF16),
+            dma((7, 3)),
+            dma((7, 3)),
+            vm((PARTS, 64, 16, 128), BF16),
+            vm((PARTS, 7, 8, 16, 128), BF16),
+            vm((PARTS, 8, 16, 128), BF16),
+            vm((PARTS, 7, 16, 128), BF16),
+            dma((PARTS, 4, 7)),
+            dma((PARTS, 4, 7)),
+        ],
+        compiler_params=pltpu.CompilerParams(
+            collective_id=0, has_side_effects=True, vmem_limit_bytes=56 * 2**20
+        ),
+    )(*inputs)
+    conv, encode, head, velocity_next = pl.pallas_call(
+        finish_kernel,
+        name="finish",
         out_shape=(
             shaped((CONV_ROWS, 256), F32),
             shaped((64, 1024), F32),
             shaped((64, 128), F32),
+            shaped((3, 256, 512), F32),
         ),
-        in_specs=[VM],
-        out_specs=(VM, VM, VM),
-        scratch_shapes=[
-            pltpu.VMEM((GRAD_ROWS, 256), BF16),
-            pltpu.VMEM((3, 512, 256), BF16),
-            pltpu.VMEM((512, 256), BF16),
-            pltpu.VMEM((7, 64, 256), BF16),
-            pltpu.VMEM((64, 256), BF16),
-            pltpu.VMEM((32, 256), BF16),
-            pltpu.VMEM((512, 256), F32),
-            pltpu.VMEM((64, 256), F32),
-            pltpu.VMEM((GRAD_ROWS, 256), BF16),
-            dma((22,)),
-            dma((22,)),
-        ],
-        compiler_params=pltpu.CompilerParams(
-            collective_id=2, has_side_effects=True, vmem_limit_bytes=32 * 2**20
-        ),
-    )(grads)
-
-
-def body(velocity, slot_of, w_encode, w_conv, w_head):
-    wide, narrow, select, unselect, bottom = element_tables(NP)
-    dma = pltpu.SemaphoreType.DMA
-    flow = pl.pallas_call(
-        lambda *refs: flow_kernel(lax.axis_size("sim"), *refs),
-        name="flow",
-        out_shape=(
-            shaped((3, 256, 512), F32),
-            shaped((4, 64, 256), BF16),
-            shaped((256, 256), F32),
-            shaped((256, 1024), BF16),
-            shaped((4, 64, 128), BF16),
-        ),
-        in_specs=[VM] * 8,
-        out_specs=(VM,) * 5,
-        scratch_shapes=[
-            pltpu.VMEM((256, 256), F32),
-            pltpu.VMEM((2, 3, 256, 512), F32),
-            pltpu.VMEM((3, 256, 512), F32),
-            pltpu.VMEM((3, 256, 384), F32),
-            pltpu.VMEM((STEPS, 2, 3, 128, 128), BF16),
-            pltpu.VMEM((STEPS, 2, 3, 64, 128), BF16),
-            pltpu.VMEM((STEPS, 2, 3, 128, 128), BF16),
-            pltpu.VMEM((STEPS, 2, 3, 64, 128), BF16),
-            dma((STEPS, 4)),
-            dma((STEPS, 4)),
-        ],
-        compiler_params=pltpu.CompilerParams(
-            collective_id=0, has_side_effects=True, vmem_limit_bytes=48 * 2**20
-        ),
-    )
-    velocity_next, h1, z1, snapshot, target = flow(
-        velocity[0, 0], slot_of[0], wide, narrow, select, unselect, bottom, w_encode
-    )
-    train = pl.pallas_call(
-        train_kernel,
-        name="train",
-        out_shape=shaped((GRAD_ROWS, 256), F32),
-        in_specs=[VM] * 6,
-        out_specs=VM,
-        scratch_shapes=[
-            pltpu.VMEM((4, 64, 256), BF16),
-            pltpu.VMEM((4, 64, 128), BF16),
-            pltpu.VMEM((4, 4, 64, 256), BF16),
-            pltpu.VMEM((9, 288, 256), BF16),
-            pltpu.VMEM((2, 256, 128), BF16),
-            pltpu.VMEM((4, 256, 128), BF16),
-            pltpu.VMEM((9, 4, 288, 128), BF16),
-            pltpu.VMEM((9, 4, 288, 128), BF16),
-            pltpu.VMEM((1024, 512), BF16),
-            pltpu.VMEM((4, 64, 256), BF16),
-            pltpu.VMEM((4, 64, 256), BF16),
-            pltpu.VMEM((4, 256, 256), F32),
-            pltpu.VMEM((2, 3, 4, 64, 256), BF16),
-            pltpu.VMEM((4, 64, 128), BF16),
-            pltpu.VMEM((3, 64, 128), BF16),
-            dma((7, 3)),
-            dma((7, 3)),
-        ],
-        compiler_params=pltpu.CompilerParams(
-            collective_id=1, has_side_effects=True, vmem_limit_bytes=48 * 2**20
-        ),
-    )
-    grads = train(h1, target, z1, snapshot, w_conv, w_head)
-    conv, encode, head = reduced(grads)
+        in_specs=[VM, VM],
+        out_specs=(VM, VM, VM, VM),
+        compiler_params=pltpu.CompilerParams(vmem_limit_bytes=16 * 2**20),
+    )(result, velocity_next)
     return (
         velocity_next[None, None],
         encode.T,

time: 114 us -> 83.9 us (0.74)
  the two profiles are of different devices: /device:TPU:64 before, /device:TPU:24 now
where the time goes in v2:
time: 83.9 us; the launch traced here: 83.7 us
  Pallas kernels  80.5 us (96%)
  local copies, waits for them, and re-layouts  2.63 us (3%)
    pallas_call x1, Pallas kernels, body(): pl.pallas_call(lambda *refs: step_kernel(lax.axis_size('sim'), *refs), na...  78.5 us
    unnamed x4, local copies, waits for them, and re-layouts  2.63 us
    pallas_call x1, Pallas kernels, body(): pl.pallas_call(finish_kernel, name='finish', out_shape=(shaped((CONV_ROWS...  1.93 us

profile of v2, /device:TPU:24, one launch (start us, length us, event | category | flops | bytes accessed | tf_op | source)
XLA Modules:
  0.0 83.7 jit_solution(8504069957820712728)
XLA Ops:
  0.6 78.5 %step.1 = (f32[3,256,512]{2,1,0:T(8,128)}, bf16[4,64,16,128]{3,2,1,0:T(8,128)(2,1)}) custom-call(f32[3,256,512]{2,1,0:T(8,128)} %bitcast.7, s32[1,256]{1,0:T(1,128)} %bitcast.8, bf16[512,1024]{1,0:T(8,128)(2,1)} %constant.10.clone.refs_2_, bf16[256,512]{1,0:T(8,128)(2,1)} %constant.11.clone.refs_3_, bf16[512,384]{1,0:T(8,128)(2,1)} %constant.12.clone.refs_4_, ...), custom_call_target="tpu_custom_call" | custom-call | tf_op jit(solution)/shard_map/step/pallas_call | solution.py:585
  79.2 0.0 copy-start
  79.2 1.4 %copy-done = f32[3,256,512]{2,1,0:T(8,128)S(1)} copy-done((f32[3,256,512]{2,1,0:T(8,128)S(1)}, f32[3,256,512]{2,1,0:T(8,128)}, u32[]{:S(2)}) %copy-start) | copy-done | bytes 1572888
  80.6 0.0 copy-start.1
  80.6 1.2 %copy-done.1 = bf16[4,64,16,128]{3,2,1,0:T(8,128)(2,1)S(1)} copy-done((bf16[4,64,16,128]{3,2,1,0:T(8,128)(2,1)S(1)}, bf16[4,64,16,128]{3,2,1,0:T(8,128)(2,1)}, u32[]{:S(2)}) %copy-start.1) | copy-done | bytes 1048600
  81.8 1.9 %finish.1 = (f32[1728,256]{1,0:T(8,128)}, f32[64,1024]{1,0:T(8,128)}, f32[64,128]{1,0:T(8,128)}, f32[3,256,512]{2,1,0:T(8,128)}) custom-call(bf16[4,64,16,128]{3,2,1,0:T(8,128)(2,1)S(1)} %copy-done.1, f32[3,256,512]{2,1,0:T(8,128)S(1)} %copy-done), custom_call_target="tpu_custom_call" | custom-call | tf_op jit(solution)/shard_map/finish/pallas_call | solution.py:642
Async XLA Ops:
  79.2 1.4 %copy-start = (f32[3,256,512]{2,1,0:T(8,128)S(1)}, f32[3,256,512]{2,1,0:T(8,128)}, u32[]{:S(2)}) copy-start(f32[3,256,512]{2,1,0:T(8,128)} %get-tuple-element.11.vel_in) | copy-start | bytes 4718596
  80.6 1.2 %copy-start.1 = (bf16[4,64,16,128]{3,2,1,0:T(8,128)(2,1)S(1)}, bf16[4,64,16,128]{3,2,1,0:T(8,128)(2,1)}, u32[]{:S(2)}) copy-start(bf16[4,64,16,128]{3,2,1,0:T(8,128)(2,1)} %get-tuple-element.10.result) | copy-start | bytes 3145732

commit v3 on v2

--- a/solution.py
+++ b/solution.py
@@ -117,13 +117,6 @@
     )
 
 
-def greet(devices):
-    barrier = pltpu.get_barrier_semaphore()
-    for device in devices:
-        pl.semaphore_signal(barrier, inc=1, device_id=device, device_id_type=MESH)
-    pl.semaphore_wait(barrier, len(devices))
-
-
 def variants(value, width):
     place = lax.broadcasted_iota(jnp.int32, (32, 8, width), 1)
     flat = value.reshape(32, 8, width)
@@ -152,7 +145,8 @@
     enc_hbm,
     conv_hbm,
     head_hbm,
-    out_ref,
+    out_hbm,
+    result_hbm,
     result,
     vel_ref,
     slot_ref,
@@ -165,6 +159,7 @@
     conv_ref,
     head_ref,
     load_sem,
+    store_sem,
     perm,
     field,
     partial,
@@ -176,11 +171,11 @@
     halo_send,
     halo_recv,
     h1_ref,
-    z1_ref,
     snap_ref,
     target_ref,
     crop_h,
     crop_t,
+    crop_s,
     all_h,
     shifted,
     dz2_buf,
@@ -188,8 +183,6 @@
     shifted_low,
     shifted_high,
     taps,
-    dh1_buf,
-    all_dh1,
     enc_buf,
     enc_out,
     all_enc,
@@ -207,24 +200,25 @@
     sim = lax.axis_index("sim")
     grp = lax.axis_index("grp")
 
-    loads = []
-    for k, (src, dst) in enumerate(
-        [
-            (slot_hbm, slot_ref),
-            (vel_hbm, vel_ref),
-            (sel_hbm, sel_ref),
-            (wide_hbm, wide_ref),
-            (narrow_hbm, narrow_ref),
-            (unsel_hbm, unsel_ref),
-            (enc_hbm, enc_ref),
-            (bottom_hbm, bottom_ref),
-            (conv_hbm, conv_ref),
-            (head_hbm, head_ref),
-        ]
-    ):
-        copy = pltpu.make_async_copy(src, dst, load_sem.at[k])
+    sources = [
+        (slot_hbm, slot_ref),
+        (vel_hbm.at[0], vel_ref.at[0]),
+        (vel_hbm.at[1], vel_ref.at[1]),
+        (vel_hbm.at[2], vel_ref.at[2]),
+        (sel_hbm, sel_ref),
+        (wide_hbm, wide_ref),
+        (narrow_hbm, narrow_ref),
+        (unsel_hbm, unsel_ref),
+        (enc_hbm, enc_ref),
+        (bottom_hbm, bottom_ref),
+        (conv_hbm, conv_ref),
+        (head_hbm, head_ref),
+    ]
+    loads = [
+        pltpu.make_async_copy(src, dst, load_sem.at[k]) for k, (src, dst) in enumerate(sources)
+    ]
+    for copy in loads[:8]:
         copy.start()
-        loads.append(copy)
 
     right = (lax.rem(sim + 1, sims), grp)
     left = (lax.rem(sim + sims - 1, sims), grp)
@@ -236,7 +230,10 @@
     peers_depth = [lax.rem(depth + d, 8) for d in range(1, 8)]
     dev_plane = [(p * 8 + depth, grp) for p in peers_plane]
     dev_depth = [(plane * 8 + p, grp) for p in peers_depth]
-    greet([left, right] + [(sim, peer) for peer in peers] + dev_plane + dev_depth)
+    friends = [left, right] + [(sim, peer) for peer in peers] + dev_plane + dev_depth
+    barrier = pltpu.get_barrier_semaphore()
+    for device in friends:
+        pl.semaphore_signal(barrier, inc=1, device_id=device, device_id_type=MESH)
 
     loads[0].wait()
     owner = lax.broadcasted_iota(jnp.int32, (256, 256), 0)
@@ -249,11 +246,13 @@
                 new = j * 64 + iy * 16 + ix * 8
                 perm[new : new + 8] = by_place[old : old + 8]
     gather = perm[...].astype(BF16)
-    loads[1].wait()
+    for copy in loads[8:]:
+        copy.start()
     for c in range(3):
+        loads[1 + c].wait()
         high, low = parts(vel_ref[c])
         field[0, c] = dot(gather, high) + dot(gather, low)
-    for copy in loads[2:6]:
+    for copy in loads[4:8]:
         copy.wait()
 
     for step in range(STEPS):
@@ -266,6 +265,8 @@
             send_x[step, 1, c] = along_x[:, 0].reshape(128, 128).astype(BF16)
             send_y[step, 0, c] = along_y[:, 3].reshape(64, 128).astype(BF16)
             send_y[step, 1, c] = along_y[:, 0].reshape(64, 128).astype(BF16)
+        if step == 0:
+            pl.semaphore_wait(barrier, len(friends))
         copies = []
         for k, (src, dst, device) in enumerate(
             [
@@ -327,9 +328,9 @@
                 )
 
     final = STEPS % 2
-    snap_ref[:, 0:512] = field[final, 0].astype(BF16)
-    snap_ref[:, 512:1024] = field[final, 2].astype(BF16)
-    for copy in loads[6:]:
+    snap_ref[:, :, 0:512] = field[final, 0].astype(BF16).reshape(4, 64, 512)
+    snap_ref[:, :, 512:1024] = field[final, 2].astype(BF16).reshape(4, 64, 512)
+    for copy in loads[8:10]:
         copy.wait()
 
     def block(index):
@@ -343,8 +344,7 @@
             copies.append(copy)
         return copies
 
-    z1 = dot(snap_ref[...], enc_ref[...])
-    z1_ref[...] = z1
+    z1 = dot(snap_ref[...].reshape(256, 1024), enc_ref[...])
     h1_ref[...] = (z1 * jax.nn.sigmoid(z1)).astype(BF16).reshape(4, 64, 256)
     h_copies = exchange(0, [(h1_ref.at[p], crop_h.at[grp]) for p in peers])
     table_high, table_low = parts(bottom_ref[...])
@@ -356,9 +356,19 @@
     both = jnp.where(lanes_low((256, 128)), stress[0], side).astype(BF16)
     target_ref[...] = both.reshape(4, 64, 128)
     t_copies = exchange(1, [(target_ref.at[p], crop_t.at[grp]) for p in peers])
-    a_copies = exchange(2, [(h1_ref, all_h.at[:, grp]) for p in peers])
+    s_copies = exchange(5, [(snap_ref.at[p], crop_s.at[grp]) for p in peers])
+    mate = grp + 1 - 2 * lax.rem(grp, 2)
+    across = lax.rem(grp + 2, 4)
+    a_copies = []
+    for d, p in enumerate((mate, across)):
+        copy = remote(
+            h1_ref, all_h.at[:, grp], grp_send.at[2, d], grp_recv.at[2, d], (sim, p)
+        )
+        copy.start()
+        a_copies.append(copy)
     crop_h[grp] = h1_ref[grp]
     crop_t[grp] = target_ref[grp]
+    crop_s[grp] = snap_ref[grp]
     all_h[:, grp] = h1_ref[...]
     for k in range(9):
         shifted[k, 0:16] = jnp.zeros((16, 256), BF16)
@@ -371,22 +381,37 @@
     scatter = perm[...].T.astype(BF16)
     for c in range(3):
         high, low = parts(field[final, c])
-        out_ref[c] = dot(scatter, high) + dot(scatter, low)
+        vel_ref[c] = dot(scatter, high) + dot(scatter, low)
+    stores = [pltpu.make_async_copy(vel_ref, out_hbm, store_sem.at[0])]
+    stores[0].start()
 
     for copy in h_copies:
+        copy.wait()
+    for copy in loads[10:]:
         copy.wait()
     value = crop_h[...].reshape(256, 256).astype(F32)
     for dx, dz, moved in variants(value, 256):
         shifted[3 * (dx + 1) + dz + 1, 16:272] = moved.astype(BF16)
-    z2 = jnp.zeros((256, 256), F32)
+    sums = [jnp.zeros((256, 256), F32)] * 2
     for dx in (-1, 0, 1):
         for dy in (-1, 0, 1):
             for dz in (-1, 0, 1):
                 tap = 9 * (dx + 1) + 3 * (dy + 1) + dz + 1
                 start = 16 * (1 + dy)
-                z2 = z2 + dot(
+                sums[tap % 2] = sums[tap % 2] + dot(
                     shifted[3 * (dx + 1) + dz + 1, start : start + 256], conv_ref[tap]
                 )
+    z2 = sums[0] + sums[1]
+    a_copies[1].wait()
+    relay = remote(
+        all_h.at[:, across],
+        all_h.at[:, across],
+        grp_send.at[2, 2],
+        grp_recv.at[2, 2],
+        (sim, mate),
+    )
+    relay.start()
+    a_copies = [a_copies[0], relay]
     h2 = (z2 * jax.nn.sigmoid(z2)).astype(BF16)
     output = dot(h2, head_ref[...])
     for copy in t_copies:
@@ -403,18 +428,25 @@
 
     for dx, dz, moved in variants(dz2.astype(F32), 256):
         shifted[3 * (dx + 1) + dz + 1, 16:272] = moved.astype(BF16)
-    dh1 = jnp.zeros((256, 256), F32)
+    sums = [jnp.zeros((256, 256), F32)] * 2
     for dx in (-1, 0, 1):
         for dy in (-1, 0, 1):
             for dz in (-1, 0, 1):
                 tap = 9 * (dx + 1) + 3 * (dy + 1) + dz + 1
                 start = 16 * (1 - dy)
-                dh1 = dh1 + dot_cols(
+                sums[tap % 2] = sums[tap % 2] + dot_cols(
                     shifted[3 * (1 - dx) + 1 - dz, start : start + 256], conv_ref[tap]
                 )
-    dh1_buf[...] = dh1.astype(BF16).reshape(4, 64, 256)
-    all_dh1[grp] = dh1_buf[grp]
-    d_copies = exchange(5, [(dh1_buf.at[p], all_dh1.at[grp]) for p in peers])
+    for copy in s_copies:
+        copy.wait()
+    rows = crop_s[...].reshape(256, 1024)
+    dz1 = ((sums[0] + sums[1]) * silu_grad(dot(rows, enc_ref[...]))).astype(BF16)
+    for b in range(4):
+        enc_buf[b] = dot_rows(dz1, rows[:, b * 256 : b * 256 + 256])
+    for d, p in enumerate(peers):
+        for b in range(4):
+            enc_out[d, b] = enc_buf[b, block(p)].astype(BF16)
+    e_copies = exchange(6, [(enc_out.at[d], all_enc.at[d]) for d in range(3)])
 
     for copy in z_copies:
         copy.wait()
@@ -506,18 +538,15 @@
             ]
         if phase < 4:
             flying[part] = spread(part, phase, triples)
+        else:
+            copy = pltpu.make_async_copy(
+                result.at[part], result_hbm.at[part], store_sem.at[1 + part]
+            )
+            copy.start()
+            stores.append(copy)
 
     conv_grad(0)
     advance(0, 0)
-    for copy in d_copies:
-        copy.wait()
-    dz1 = (all_dh1[...].reshape(256, 256).astype(F32) * silu_grad(z1_ref[...])).astype(BF16)
-    for b in range(4):
-        enc_buf[b] = dot_rows(dz1, snap_ref[:, b * 256 : b * 256 + 256])
-    for d, p in enumerate(peers):
-        for b in range(4):
-            enc_out[d, b] = enc_buf[b, block(p)].astype(BF16)
-    e_copies = exchange(6, [(enc_out.at[d], all_enc.at[d]) for d in range(3)])
     conv_grad(1)
     advance(1, 0)
     conv_grad(2)
@@ -544,6 +573,8 @@
     advance(3, 0)
     for part, phase in ORDER:
         advance(part, phase)
+    for copy in stores:
+        copy.wait()
 
 
 ORDER = [
@@ -552,14 +583,46 @@
 ]
 
 
-def finish_kernel(result, vel_in, conv_ref, enc_ref, head_ref, vel_ref):
-    vel_ref[...] = vel_in[...]
+def finish_kernel(
+    result_hbm,
+    vel_in,
+    conv_hbm,
+    enc_hbm,
+    head_hbm,
+    vel_out,
+    result,
+    vel_ref,
+    conv_ref,
+    enc_ref,
+    head_ref,
+    load_sem,
+    store_sem,
+):
+    loads = [
+        pltpu.make_async_copy(result_hbm.at[part], result.at[part], load_sem.at[part])
+        for part in range(PARTS)
+    ]
+    loads.append(pltpu.make_async_copy(vel_in, vel_ref, load_sem.at[PARTS]))
+    for copy in loads:
+        copy.start()
+    stores = []
+
+    def store(src, dst):
+        copy = pltpu.make_async_copy(src, dst, store_sem.at[len(stores)])
+        copy.start()
+        stores.append(copy)
+
     for part in range(PARTS):
+        loads[part].wait()
         count = min(512, CONV_ROWS - 512 * part)
         for half in range(2):
             lanes = slice(128 * half, 128 * half + 128)
             value = result[part, 32 * half : 32 * half + count // 16].astype(F32)
             conv_ref[512 * part : 512 * part + count, lanes] = value.reshape(count, 128)
+        span = pl.ds(512 * part, count)
+        store(conv_ref.at[span], conv_hbm.at[span])
+    loads[PARTS].wait()
+    store(vel_ref, vel_out)
     for half in range(2):
         for b in range(4):
             place = 32 * half + 12 + 4 * b
@@ -567,6 +630,10 @@
             enc_ref[:, 256 * b + 128 * half : 256 * b + 128 * half + 128] = value
         value = result[3, 32 * half + 28 : 32 * half + 30].astype(F32).reshape(32, 128)
         head_ref[32 * half : 32 * half + 32] = value
+    store(enc_ref, enc_hbm)
+    store(head_ref, head_hbm)
+    for copy in stores:
+        copy.wait()
 
 
 VM = pl.BlockSpec(memory_space=pltpu.VMEM)
@@ -587,15 +654,17 @@
         name="step",
         out_shape=(shaped((3, 256, 512), F32), shaped((PARTS, 64, 16, 128), BF16)),
         in_specs=[HB] * len(inputs),
-        out_specs=(VM, VM),
+        out_specs=(HB, HB),
         scratch_shapes=[
+            vm((PARTS, 64, 16, 128), BF16),
             vm((3, 256, 512), F32),
             vm((1, 256), jnp.int32),
             *[vm(table.shape, table.dtype) for table in tables],
             vm((1024, 256), BF16),
             vm((27, 256, 256), BF16),
             vm((256, 128), BF16),
-            dma((len(inputs),)),
+            dma((len(inputs) + 2,)),
+            dma((1 + PARTS,)),
             vm((256, 256), F32),
             vm((2, 3, 256, 512), F32),
             vm((3, 256, 512), F32),
@@ -607,11 +676,11 @@
             dma((STEPS, 4)),
             dma((STEPS, 4)),
             vm((4, 64, 256), BF16),
-            vm((256, 256), F32),
-            vm((256, 1024), BF16),
+            vm((4, 64, 1024), BF16),
             vm((4, 64, 128), BF16),
             vm((4, 64, 256), BF16),
             vm((4, 64, 128), BF16),
+            vm((4, 64, 1024), BF16),
             vm((4, 4, 64, 256), BF16),
             vm((9, 288, 256), BF16),
             vm((2, 256, 128), BF16),
@@ -619,8 +688,6 @@
             vm((9, 4, 288, 128), BF16),
             vm((9, 4, 288, 128), BF16),
             vm((1024, 512), BF16),
-            vm((4, 64, 256), BF16),
-            vm((4, 64, 256), BF16),
             vm((4, 256, 256), F32),
             vm((3, 4, 64, 256), BF16),
             vm((3, 4, 64, 256), BF16),
@@ -636,7 +703,7 @@
             dma((PARTS, 4, 7)),
         ],
         compiler_params=pltpu.CompilerParams(
-            collective_id=0, has_side_effects=True, vmem_limit_bytes=56 * 2**20
+            collective_id=0, has_side_effects=True, vmem_limit_bytes=62 * 2**20
         ),
     )(*inputs)
     conv, encode, head, velocity_next = pl.pallas_call(
@@ -648,9 +715,18 @@
             shaped((64, 128), F32),
             shaped((3, 256, 512), F32),
         ),
-        in_specs=[VM, VM],
-        out_specs=(VM, VM, VM, VM),
-        compiler_params=pltpu.CompilerParams(vmem_limit_bytes=16 * 2**20),
+        in_specs=[HB, HB],
+        out_specs=(HB, HB, HB, HB),
+        scratch_shapes=[
+            vm((PARTS, 64, 16, 128), BF16),
+            vm((3, 256, 512), F32),
+            vm((CONV_ROWS, 256), F32),
+            vm((64, 1024), F32),
+            vm((64, 128), F32),
+            dma((PARTS + 1,)),
+            dma((PARTS + 3,)),
+        ],
+        compiler_params=pltpu.CompilerParams(vmem_limit_bytes=62 * 2**20),
     )(result, velocity_next)
     return (
         velocity_next[None, None],

time: 83.9 us -> 83.8 us (level)
  local copies, waits for them, and re-layouts: 2.63 us -> 0 us
  Pallas kernels: 80.5 us -> 82.1 us
    unnamed x4 -> x0, local copies, waits for them, and re-layouts: 2.63 us -> none
    pallas_call x1, Pallas kernels: 1.93 us -> 3.07 us  [body(): pl.pallas_call(finish_kernel, name='finish', out_shape=(shaped((CONV_ROWS...]
where the time goes in v3:
time: 83.8 us; the launch traced here: 82.9 us
  Pallas kernels  82.1 us (98%)
    pallas_call x1, Pallas kernels, body(): pl.pallas_call(lambda *refs: step_kernel(lax.axis_size('sim'), *refs), na...  79.1 us
    pallas_call x1, Pallas kernels, body(): pl.pallas_call(finish_kernel, name='finish', out_shape=(shaped((CONV_ROWS...  3.07 us

profile of v3, /device:TPU:24, one launch (start us, length us, event | category | flops | bytes accessed | tf_op | source)
XLA Modules:
  0.0 82.9 jit_solution(271056147610229009)
XLA Ops:
  0.6 79.1 %step.1 = (f32[3,256,512]{2,1,0:T(8,128)}, bf16[4,64,16,128]{3,2,1,0:T(8,128)(2,1)}) custom-call(f32[3,256,512]{2,1,0:T(8,128)} %bitcast.7, s32[1,256]{1,0:T(1,128)} %bitcast.8, bf16[512,1024]{1,0:T(8,128)(2,1)} %constant.10.clone.refs_2_, bf16[256,512]{1,0:T(8,128)(2,1)} %constant.11.clone.refs_3_, bf16[512,384]{1,0:T(8,128)(2,1)} %constant.12.clone.refs_4_, ...), custom_call_target="tpu_custom_call" | custom-call | tf_op jit(solution)/shard_map/step/pallas_call | solution.py:652
  79.7 3.1 %finish.1 = (f32[1728,256]{1,0:T(8,128)}, f32[64,1024]{1,0:T(8,128)}, f32[64,128]{1,0:T(8,128)}, f32[3,256,512]{2,1,0:T(8,128)}) custom-call(bf16[4,64,16,128]{3,2,1,0:T(8,128)(2,1)} %get-tuple-element.10.result_hbm, f32[3,256,512]{2,1,0:T(8,128)} %get-tuple-element.11.vel_in), custom_call_target="tpu_custom_call" | custom-call | tf_op jit(solution)/shard_map/finish/pallas_call | solution.py:709

commit v4 on v3

--- a/solution.py
+++ b/solution.py
@@ -19,7 +19,7 @@
 BF16 = jnp.bfloat16
 
 CONV_ROWS = 1728
-PARTS = 4
+PARTS = 3
 
 
 def derivative_matrix(count):
@@ -147,6 +147,8 @@
     head_hbm,
     out_hbm,
     result_hbm,
+    small_hbm,
+    enc_grad_hbm,
     result,
     vel_ref,
     slot_ref,
@@ -171,11 +173,11 @@
     halo_send,
     halo_recv,
     h1_ref,
+    z1_ref,
     snap_ref,
     target_ref,
     crop_h,
     crop_t,
-    crop_s,
     all_h,
     shifted,
     dz2_buf,
@@ -183,9 +185,11 @@
     shifted_low,
     shifted_high,
     taps,
+    dh1_buf,
+    all_dh1,
     enc_buf,
     enc_out,
-    all_enc,
+    enc_in,
     head_buf,
     all_head,
     grp_send,
@@ -196,6 +200,18 @@
     recv_second,
     sum_send,
     sum_recv,
+    small,
+    small_recv,
+    small_piece,
+    small_layers,
+    small_ready,
+    enc_half,
+    enc_recv,
+    enc_piece,
+    enc_layers,
+    enc_ready,
+    tail_send,
+    tail_recv,
 ):
     sim = lax.axis_index("sim")
     grp = lax.axis_index("grp")
@@ -230,7 +246,14 @@
     peers_depth = [lax.rem(depth + d, 8) for d in range(1, 8)]
     dev_plane = [(p * 8 + depth, grp) for p in peers_plane]
     dev_depth = [(plane * 8 + p, grp) for p in peers_depth]
-    friends = [left, right] + [(sim, peer) for peer in peers] + dev_plane + dev_depth
+    mate = grp + 1 - 2 * lax.rem(grp, 2)
+    across = lax.rem(grp + 2, 4)
+    wide_plane = [
+        (lax.rem(plane + d, 8) * 8 + depth, across if turn else grp)
+        for turn in (0, 1)
+        for d in range(8)
+    ][1:]
+    friends = [left, right, (sim, mate), (sim, lax.rem(mate + 2, 4))] + wide_plane + dev_depth
     barrier = pltpu.get_barrier_semaphore()
     for device in friends:
         pl.semaphore_signal(barrier, inc=1, device_id=device, device_id_type=MESH)
@@ -328,8 +351,8 @@
                 )
 
     final = STEPS % 2
-    snap_ref[:, :, 0:512] = field[final, 0].astype(BF16).reshape(4, 64, 512)
-    snap_ref[:, :, 512:1024] = field[final, 2].astype(BF16).reshape(4, 64, 512)
+    snap_ref[:, 0:512] = field[final, 0].astype(BF16)
+    snap_ref[:, 512:1024] = field[final, 2].astype(BF16)
     for copy in loads[8:10]:
         copy.wait()
 
@@ -344,7 +367,8 @@
             copies.append(copy)
         return copies
 
-    z1 = dot(snap_ref[...].reshape(256, 1024), enc_ref[...])
+    z1 = dot(snap_ref[...], enc_ref[...])
+    z1_ref[...] = z1
     h1_ref[...] = (z1 * jax.nn.sigmoid(z1)).astype(BF16).reshape(4, 64, 256)
     h_copies = exchange(0, [(h1_ref.at[p], crop_h.at[grp]) for p in peers])
     table_high, table_low = parts(bottom_ref[...])
@@ -356,9 +380,6 @@
     both = jnp.where(lanes_low((256, 128)), stress[0], side).astype(BF16)
     target_ref[...] = both.reshape(4, 64, 128)
     t_copies = exchange(1, [(target_ref.at[p], crop_t.at[grp]) for p in peers])
-    s_copies = exchange(5, [(snap_ref.at[p], crop_s.at[grp]) for p in peers])
-    mate = grp + 1 - 2 * lax.rem(grp, 2)
-    across = lax.rem(grp + 2, 4)
     a_copies = []
     for d, p in enumerate((mate, across)):
         copy = remote(
@@ -368,7 +389,6 @@
         a_copies.append(copy)
     crop_h[grp] = h1_ref[grp]
     crop_t[grp] = target_ref[grp]
-    crop_s[grp] = snap_ref[grp]
     all_h[:, grp] = h1_ref[...]
     for k in range(9):
         shifted[k, 0:16] = jnp.zeros((16, 256), BF16)
@@ -419,10 +439,17 @@
     target = crop_t[...].reshape(256, 128).astype(F32)
     resid = ((output - target) * (LOSS_WEIGHT / 65536.0)).astype(BF16)
     dz2 = (dot_cols(resid, head_ref[...]) * silu_grad(z2)).astype(BF16)
-    dz2_buf[0] = dz2[:, 0:128]
-    dz2_buf[1] = dz2[:, 128:256]
-    all_dz2[grp] = dz2_buf[grp // 2]
-    z_copies = exchange(3, [(dz2_buf.at[p // 2], all_dz2.at[grp]) for p in peers])
+    low = lanes_low((128, 128))
+    for j in range(4):
+        lanes = slice(128 * (j // 2), 128 * (j // 2) + 128)
+        upper, under = dz2[0:128, lanes].astype(F32), dz2[128:256, lanes].astype(F32)
+        if j % 2 == 0:
+            packed = jnp.where(low, upper, pltpu.roll(under, 64, 1))
+        else:
+            packed = jnp.where(low, pltpu.roll(upper, 64, 1), under)
+        dz2_buf[j] = packed.astype(BF16)
+    all_dz2[grp] = dz2_buf[grp]
+    z_copies = exchange(3, [(dz2_buf.at[p], all_dz2.at[grp]) for p in peers])
     head_buf[...] = dot_rows(h2, resid).astype(BF16).reshape(4, 64, 128)
     g_copies = exchange(4, [(head_buf.at[p], all_head.at[d]) for d, p in enumerate(peers)])
 
@@ -437,29 +464,23 @@
                 sums[tap % 2] = sums[tap % 2] + dot_cols(
                     shifted[3 * (1 - dx) + 1 - dz, start : start + 256], conv_ref[tap]
                 )
-    for copy in s_copies:
-        copy.wait()
-    rows = crop_s[...].reshape(256, 1024)
-    dz1 = ((sums[0] + sums[1]) * silu_grad(dot(rows, enc_ref[...]))).astype(BF16)
-    for b in range(4):
-        enc_buf[b] = dot_rows(dz1, rows[:, b * 256 : b * 256 + 256])
-    for d, p in enumerate(peers):
-        for b in range(4):
-            enc_out[d, b] = enc_buf[b, block(p)].astype(BF16)
-    e_copies = exchange(6, [(enc_out.at[d], all_enc.at[d]) for d in range(3)])
+    dh1_buf[...] = (sums[0] + sums[1]).astype(BF16).reshape(4, 64, 256)
+    all_dh1[grp] = dh1_buf[grp]
+    d_copies = exchange(5, [(dh1_buf.at[p], all_dh1.at[grp]) for p in peers])
 
     for copy in z_copies:
         copy.wait()
-    low = lanes_low((256, 128))
     for j in range(4):
         value = all_dz2[j].astype(F32)
         turned = pltpu.roll(value, 64, 1)
-        first = lax.rem(grp, 2) == 0
-        here = jnp.where(low, jnp.where(first, value, turned), jnp.where(first, turned, value))
+        here = jnp.concatenate(
+            [jnp.where(low, value, turned), jnp.where(low, turned, value)], axis=0
+        )
         for dx, dz, moved in variants(here, 128):
             k = 3 * (dx + 1) + dz + 1
-            shifted_low[k, j, 16:272] = jnp.where(low, moved, 0.0).astype(BF16)
-            shifted_high[k, j, 16:272] = jnp.where(low, 0.0, moved).astype(BF16)
+            side = lanes_low((256, 128))
+            shifted_low[k, j, 16:272] = jnp.where(side, moved, 0.0).astype(BF16)
+            shifted_high[k, j, 16:272] = jnp.where(side, 0.0, moved).astype(BF16)
     for copy in a_copies:
         copy.wait()
 
@@ -479,7 +500,12 @@
                 taps[j * 256 : j * 256 + 256, place * 128 : place * 128 + 128] = value
         width = 128 * len(pairs)
         grad = dot_rows(taps[:, 0:width], all_h[...].reshape(1024, 256)).astype(BF16)
-        count = min(512, CONV_ROWS - 512 * part)
+        if part == PARTS:
+            for half in range(2):
+                lanes = slice(128 * half, 128 * half + 128)
+                small[half * 3 : half * 3 + 3] = grad[0:192, lanes].reshape(3, 4, 16, 128)
+            return
+        count = 512
         for half in range(2):
             work[part, 32 * half : 32 * half + count // 16] = grad[
                 0:count, 128 * half : 128 * half + 128
@@ -497,7 +523,7 @@
 
     depth_way = (depth, peers_depth, dev_depth)
     plane_way = (plane, peers_plane, dev_plane)
-    ways = [(depth_way, plane_way)] + [(plane_way, depth_way)] * (PARTS - 1)
+    ways = [(depth_way, plane_way)] + [(plane_way, depth_way)] * 2
     flying = {}
 
     def eight(index):
@@ -545,52 +571,147 @@
             copy.start()
             stores.append(copy)
 
-    conv_grad(0)
-    advance(0, 0)
-    conv_grad(1)
-    advance(1, 0)
-    conv_grad(2)
-    advance(2, 0)
-    advance(0, 1)
-    conv_grad(3)
-    for copy in e_copies + g_copies:
-        copy.wait()
-    for b in range(4):
-        total = enc_buf[b, block(grp)]
-        for d in range(3):
-            total = total + all_enc[d, b].astype(F32)
-        total = total.astype(BF16)
-        for half in range(2):
-            place = 32 * half + 12 + 4 * b
-            work[3, place : place + 4] = total[:, 128 * half : 128 * half + 128].reshape(4, 16, 128)
+    tail = {}
+
+    def settle(which, phase):
+        piece, layers, ready = tails[which]
+        if phase > 0:
+            for copy in tail[which]:
+                copy.wait()
+
+        def spread_small(triples):
+            copies = []
+            for d, (src, dst, device) in enumerate(triples):
+                copy = remote(
+                    src,
+                    dst,
+                    tail_send.at[which, phase, d],
+                    tail_recv.at[which, phase, d],
+                    device,
+                )
+                copy.start()
+                copies.append(copy)
+            return copies
+
+        if phase == 0:
+            if which == 0:
+                tail[which] = spread_small(
+                    [
+                        (small.at[peers_plane[d]], small_recv.at[d], dev_plane[d])
+                        for d in range(7)
+                    ]
+                )
+            else:
+                triples = []
+                for turn in (0, 1):
+                    side = lax.rem(grp // 2 + turn, 2)
+                    for d in range(8):
+                        if turn or d:
+                            triples.append(
+                                (
+                                    enc_half.at[side, lax.rem(plane + d, 8)],
+                                    enc_recv.at[8 * turn + d - 1],
+                                    wide_plane[8 * turn + d - 1],
+                                )
+                            )
+                tail[which] = spread_small(triples)
+        if phase == 1:
+            if which == 0:
+                total = small[plane].astype(F32)
+                for d in range(7):
+                    total = total + small_recv[d].astype(F32)
+            else:
+                total = enc_half[grp // 2, plane].astype(F32)
+                for d in range(15):
+                    total = total + enc_recv[d].astype(F32)
+            piece[...] = total.astype(BF16)
+            layers[depth] = piece[...]
+            tail[which] = spread_small(
+                [(piece, layers.at[depth], dev_depth[d]) for d in range(7)]
+            )
+        if phase == 2:
+            total = layers[0].astype(F32)
+            for d in range(1, 8):
+                total = total + layers[d].astype(F32)
+            ready[plane] = total.astype(BF16)
+            tail[which] = spread_small(
+                [(ready.at[plane], ready.at[plane], dev_plane[d]) for d in range(7)]
+            )
+        if phase == 3:
+            copy = pltpu.make_async_copy(
+                ready, (small_hbm, enc_grad_hbm)[which], store_sem.at[1 + PARTS + which]
+            )
+            copy.start()
+            stores.append(copy)
+
+    tails = (
+        (small_piece, small_layers, small_ready),
+        (enc_piece, enc_layers, enc_ready),
+    )
+
+    for part in range(PARTS):
+        conv_grad(part)
+        advance(part, 0)
+    conv_grad(PARTS)
+    for copy in g_copies:
+        copy.wait()
     total = head_buf[grp].astype(F32)
     for d in range(3):
         total = total + all_head[d].astype(F32)
-    total = total.astype(BF16).reshape(4, 16, 128)
-    for half in range(2):
-        work[3, 32 * half + 28 : 32 * half + 30] = total[2 * half : 2 * half + 2]
-        work[3, 32 * half + 30 : 32 * half + 32] = jnp.zeros((2, 16, 128), BF16)
-    advance(3, 0)
+    small[6] = total.astype(BF16).reshape(4, 16, 128)
+    small[7] = jnp.zeros((4, 16, 128), BF16)
+    settle(0, 0)
+
+    for copy in d_copies:
+        copy.wait()
+    dz1 = (all_dh1[...].reshape(256, 256).astype(F32) * silu_grad(z1_ref[...])).astype(BF16)
+    for b in range(4):
+        grad = dot_rows(dz1, snap_ref[:, b * 256 : b * 256 + 256])
+        enc_buf[:, b] = grad.reshape(4, 64, 256)
+    theirs = lax.rem(mate, 2)
+    ours = lax.rem(grp, 2)
+    for side in range(2):
+        enc_out[side] = enc_buf[2 * side + theirs].astype(BF16)
+    m_copy = remote(enc_out, enc_in, grp_send.at[6, 0], grp_recv.at[6, 0], (sim, mate))
+    m_copy.start()
+    m_copy.wait()
+    for side in range(2):
+        for b in range(4):
+            total = enc_buf[2 * side + ours, b] + enc_in[side, b].astype(F32)
+            for half in range(2):
+                enc_half[side, 2 * b + half] = total[:, 128 * half : 128 * half + 128].astype(
+                    BF16
+                )
+    settle(1, 0)
     for part, phase in ORDER:
-        advance(part, phase)
+        if part < PARTS:
+            advance(part, phase)
+        else:
+            settle(part - PARTS, phase)
     for copy in stores:
         copy.wait()
 
 
 ORDER = [
-    (1, 1), (0, 2), (2, 1), (3, 1), (1, 2), (0, 3), (2, 2), (3, 2),
-    (1, 3), (2, 3), (3, 3), (0, 4), (1, 4), (2, 4), (3, 4),
+    (1, 1), (0, 1), (2, 1), (3, 1), (4, 1),
+    (1, 2), (0, 2), (2, 2), (3, 2), (4, 2),
+    (1, 3), (0, 3), (2, 3), (3, 3), (4, 3),
+    (1, 4), (0, 4), (2, 4),
 ]
 
 
 def finish_kernel(
     result_hbm,
+    small_hbm,
+    enc_grad_hbm,
     vel_in,
     conv_hbm,
     enc_hbm,
     head_hbm,
     vel_out,
     result,
+    small,
+    enc_grad,
     vel_ref,
     conv_ref,
     enc_ref,
@@ -598,11 +719,11 @@
     load_sem,
     store_sem,
 ):
+    pairs = [(result_hbm.at[part], result.at[part]) for part in range(PARTS)]
+    pairs += [(small_hbm, small), (enc_grad_hbm, enc_grad), (vel_in, vel_ref)]
     loads = [
-        pltpu.make_async_copy(result_hbm.at[part], result.at[part], load_sem.at[part])
-        for part in range(PARTS)
+        pltpu.make_async_copy(src, dst, load_sem.at[k]) for k, (src, dst) in enumerate(pairs)
     ]
-    loads.append(pltpu.make_async_copy(vel_in, vel_ref, load_sem.at[PARTS]))
     for copy in loads:
         copy.start()
     stores = []
@@ -614,24 +735,27 @@
 
     for part in range(PARTS):
         loads[part].wait()
-        count = min(512, CONV_ROWS - 512 * part)
         for half in range(2):
             lanes = slice(128 * half, 128 * half + 128)
-            value = result[part, 32 * half : 32 * half + count // 16].astype(F32)
-            conv_ref[512 * part : 512 * part + count, lanes] = value.reshape(count, 128)
-        span = pl.ds(512 * part, count)
+            value = result[part, 32 * half : 32 * half + 32].astype(F32)
+            conv_ref[512 * part : 512 * part + 512, lanes] = value.reshape(512, 128)
+        span = pl.ds(512 * part, 512)
         store(conv_ref.at[span], conv_hbm.at[span])
     loads[PARTS].wait()
+    for half in range(2):
+        lanes = slice(128 * half, 128 * half + 128)
+        value = small[3 * half : 3 * half + 3].astype(F32).reshape(192, 128)
+        conv_ref[512 * PARTS : CONV_ROWS, lanes] = value
+    span = pl.ds(512 * PARTS, 192)
+    store(conv_ref.at[span], conv_hbm.at[span])
+    head_ref[...] = small[6].astype(F32).reshape(64, 128)
+    store(head_ref, head_hbm)
+    loads[PARTS + 1].wait()
+    for b in range(8):
+        enc_ref[:, 128 * b : 128 * b + 128] = enc_grad[b].astype(F32)
+    store(enc_ref, enc_hbm)
+    loads[PARTS + 2].wait()
     store(vel_ref, vel_out)
-    for half in range(2):
-        for b in range(4):
-            place = 32 * half + 12 + 4 * b
-            value = result[3, place : place + 4].astype(F32).reshape(64, 128)
-            enc_ref[:, 256 * b + 128 * half : 256 * b + 128 * half + 128] = value
-        value = result[3, 32 * half + 28 : 32 * half + 30].astype(F32).reshape(32, 128)
-        head_ref[32 * half : 32 * half + 32] = value
-    store(enc_ref, enc_hbm)
-    store(head_ref, head_hbm)
     for copy in stores:
         copy.wait()
 
@@ -649,12 +773,17 @@
     dma = pltpu.SemaphoreType.DMA
     vm = pltpu.VMEM
     inputs = (velocity[0, 0], slot_of[0], *tables, w_encode, w_conv, w_head)
-    velocity_next, result = pl.pallas_call(
+    velocity_next, result, small, enc_grad = pl.pallas_call(
         lambda *refs: step_kernel(lax.axis_size("sim"), *refs),
         name="step",
-        out_shape=(shaped((3, 256, 512), F32), shaped((PARTS, 64, 16, 128), BF16)),
+        out_shape=(
+            shaped((3, 256, 512), F32),
+            shaped((PARTS, 64, 16, 128), BF16),
+            shaped((8, 4, 16, 128), BF16),
+            shaped((8, 64, 128), BF16),
+        ),
         in_specs=[HB] * len(inputs),
-        out_specs=(HB, HB),
+        out_specs=(HB,) * 4,
         scratch_shapes=[
             vm((PARTS, 64, 16, 128), BF16),
             vm((3, 256, 512), F32),
@@ -664,7 +793,7 @@
             vm((27, 256, 256), BF16),
             vm((256, 128), BF16),
             dma((len(inputs) + 2,)),
-            dma((1 + PARTS,)),
+            dma((3 + PARTS,)),
             vm((256, 256), F32),
             vm((2, 3, 256, 512), F32),
             vm((3, 256, 512), F32),
@@ -676,21 +805,23 @@
             dma((STEPS, 4)),
             dma((STEPS, 4)),
             vm((4, 64, 256), BF16),
-            vm((4, 64, 1024), BF16),
+            vm((256, 256), F32),
+            vm((256, 1024), BF16),
             vm((4, 64, 128), BF16),
             vm((4, 64, 256), BF16),
             vm((4, 64, 128), BF16),
-            vm((4, 64, 1024), BF16),
             vm((4, 4, 64, 256), BF16),
             vm((9, 288, 256), BF16),
-            vm((2, 256, 128), BF16),
-            vm((4, 256, 128), BF16),
+            vm((4, 128, 128), BF16),
+            vm((4, 128, 128), BF16),
             vm((9, 4, 288, 128), BF16),
             vm((9, 4, 288, 128), BF16),
             vm((1024, 512), BF16),
-            vm((4, 256, 256), F32),
-            vm((3, 4, 64, 256), BF16),
-            vm((3, 4, 64, 256), BF16),
+            vm((4, 64, 256), BF16),
+            vm((4, 64, 256), BF16),
+            vm((4, 4, 64, 256), F32),
+            vm((2, 4, 64, 256), BF16),
+            vm((2, 4, 64, 256), BF16),
             vm((4, 64, 128), BF16),
             vm((3, 64, 128), BF16),
             dma((7, 3)),
@@ -701,6 +832,18 @@
             vm((PARTS, 7, 16, 128), BF16),
             dma((PARTS, 4, 7)),
             dma((PARTS, 4, 7)),
+            vm((8, 4, 16, 128), BF16),
+            vm((7, 4, 16, 128), BF16),
+            vm((4, 16, 128), BF16),
+            vm((8, 4, 16, 128), BF16),
+            vm((8, 4, 16, 128), BF16),
+            vm((2, 8, 64, 128), BF16),
+            vm((15, 64, 128), BF16),
+            vm((64, 128), BF16),
+            vm((8, 64, 128), BF16),
+            vm((8, 64, 128), BF16),
+            dma((2, 3, 15)),
+            dma((2, 3, 15)),
         ],
         compiler_params=pltpu.CompilerParams(
             collective_id=0, has_side_effects=True, vmem_limit_bytes=62 * 2**20
@@ -715,19 +858,21 @@
             shaped((64, 128), F32),
             shaped((3, 256, 512), F32),
         ),
-        in_specs=[HB, HB],
-        out_specs=(HB, HB, HB, HB),
+        in_specs=[HB] * 4,
+        out_specs=(HB,) * 4,
         scratch_shapes=[
             vm((PARTS, 64, 16, 128), BF16),
+            vm((8, 4, 16, 128), BF16),
+            vm((8, 64, 128), BF16),
             vm((3, 256, 512), F32),
             vm((CONV_ROWS, 256), F32),
             vm((64, 1024), F32),
             vm((64, 128), F32),
-            dma((PARTS + 1,)),
             dma((PARTS + 3,)),
+            dma((PARTS + 4,)),
         ],
         compiler_params=pltpu.CompilerParams(vmem_limit_bytes=62 * 2**20),
-    )(result, velocity_next)
+    )(result, small, enc_grad, velocity_next)
     return (
         velocity_next[None, None],
         encode.T,

time: 83.8 us -> 74.2 us (0.89)
  Pallas kernels: 82.1 us -> 71.9 us
    pallas_call x1, Pallas kernels: 79.1 us -> 68.9 us  [body(): pl.pallas_call(lambda *refs: step_kernel(lax.axis_size('sim'), *refs), na...]
where the time goes in v4:
time: 74.2 us; the launch traced here: 72.7 us
  Pallas kernels  71.9 us (97%)
  between operations  0.8 us (1%)
    pallas_call x1, Pallas kernels, body(): pl.pallas_call(lambda *refs: step_kernel(lax.axis_size('sim'), *refs), na...  68.9 us
    pallas_call x1, Pallas kernels, body(): pl.pallas_call(finish_kernel, name='finish', out_shape=(shaped((CONV_ROWS...  3 us

profile of v4, /device:TPU:24, one launch (start us, length us, event | category | flops | bytes accessed | tf_op | source)
XLA Modules:
  0.0 72.7 jit_solution(13282517782452715050)
XLA Ops:
  0.6 68.9 %step.1 = (f32[3,256,512]{2,1,0:T(8,128)}, bf16[3,64,16,128]{3,2,1,0:T(8,128)(2,1)}, bf16[8,4,16,128]{3,2,1,0:T(8,128)(2,1)}, bf16[8,64,128]{2,1,0:T(8,128)(2,1)}) custom-call(f32[3,256,512]{2,1,0:T(8,128)} %bitcast.7, s32[1,256]{1,0:T(1,128)} %bitcast.8, bf16[512,1024]{1,0:T(8,128)(2,1)} %constant.10.clone.refs_2_, ...), custom_call_target="tpu_custom_call" | custom-call | tf_op jit(solution)/shard_map/step/pallas_call | solution.py:776
  69.5 3.0 %finish.1 = (f32[1728,256]{1,0:T(8,128)}, f32[64,1024]{1,0:T(8,128)}, f32[64,128]{1,0:T(8,128)}, f32[3,256,512]{2,1,0:T(8,128)}) custom-call(bf16[3,64,16,128]{3,2,1,0:T(8,128)(2,1)} %get-tuple-element.12.result_hbm, bf16[8,4,16,128]{3,2,1,0:T(8,128)(2,1)} %get-tuple-element.13.small_hbm, bf16[8,64,128]{2,1,0:T(8,128)(2,1)} %get-tuple-element.14.enc_grad_hbm, ...), custom_call_target="tpu_custom_call" | custom-call | tf_op jit(solution)/shard_map/finish/pallas_call | solution.py:852

commit v5 on v4

--- a/solution.py
+++ b/solution.py
@@ -66,7 +66,6 @@
                 )
     diffuse = TIME_STEP * VISCOSITY * (laplace.T - PENALTY * (select @ select.T))
     half = count**3 // 2
-    swapped = select.reshape(count**3, 3, 2, count * count)[:, :, ::-1].reshape(count**3, -1)
     small = lambda table: np.asarray(table, ml_dtypes.bfloat16)
     return (
         small(np.concatenate([TIME_STEP * along_x.T, diffuse], axis=1)),
@@ -75,7 +74,6 @@
             * np.concatenate([along_y.T[:half, :half], along_z.T[:half, :half]], axis=1)
         ),
         small(select),
-        small(swapped.T),
         np.asarray(bottom, np.float32),
     )
 
@@ -104,6 +102,23 @@
 
 def lanes_low(shape):
     return lax.broadcasted_iota(jnp.int32, shape, len(shape) - 1) < 64
+
+
+def packed_rows(value, high):
+    half = value.shape[0] // 2
+    turned = pltpu.roll(value[half:], 64, 1)
+    low = lanes_low((half, 128))
+    packed = jnp.where(low, turned, value[:half]) if high else jnp.where(low, value[:half], turned)
+    return packed.astype(BF16)
+
+
+def swap_halves(value):
+    return pltpu.roll(value, 64, 1).astype(BF16)
+
+
+def spread_rows(packed):
+    value = packed.astype(F32)
+    return jnp.concatenate([value, pltpu.roll(value, 64, 1)], axis=0)
 
 
 def remote(src, dst, send, recv, device):
@@ -140,7 +155,6 @@
     wide_hbm,
     narrow_hbm,
     sel_hbm,
-    unsel_hbm,
     bottom_hbm,
     enc_hbm,
     conv_hbm,
@@ -155,7 +169,6 @@
     wide_ref,
     narrow_ref,
     sel_ref,
-    unsel_ref,
     bottom_ref,
     enc_ref,
     conv_ref,
@@ -224,7 +237,6 @@
         (sel_hbm, sel_ref),
         (wide_hbm, wide_ref),
         (narrow_hbm, narrow_ref),
-        (unsel_hbm, unsel_ref),
         (enc_hbm, enc_ref),
         (bottom_hbm, bottom_ref),
         (conv_hbm, conv_ref),
@@ -233,7 +245,7 @@
     loads = [
         pltpu.make_async_copy(src, dst, load_sem.at[k]) for k, (src, dst) in enumerate(sources)
     ]
-    for copy in loads[:8]:
+    for copy in loads[:7]:
         copy.start()
 
     right = (lax.rem(sim + 1, sims), grp)
@@ -253,7 +265,7 @@
         for turn in (0, 1)
         for d in range(8)
     ][1:]
-    friends = [left, right, (sim, mate), (sim, lax.rem(mate + 2, 4))] + wide_plane + dev_depth
+    friends = dev_depth + wide_plane + [left, right, (sim, lax.rem(mate + 2, 4)), (sim, mate)]
     barrier = pltpu.get_barrier_semaphore()
     for device in friends:
         pl.semaphore_signal(barrier, inc=1, device_id=device, device_id_type=MESH)
@@ -269,39 +281,47 @@
                 new = j * 64 + iy * 16 + ix * 8
                 perm[new : new + 8] = by_place[old : old + 8]
     gather = perm[...].astype(BF16)
-    for copy in loads[8:]:
+    for copy in loads[7:]:
         copy.start()
     for c in range(3):
         loads[1 + c].wait()
         high, low = parts(vel_ref[c])
         field[0, c] = dot(gather, high) + dot(gather, low)
-    for copy in loads[4:8]:
-        copy.wait()
-
-    for step in range(STEPS):
-        now, later = step % 2, (step + 1) % 2
-        for c in range(3):
-            faces[c] = dot(field[now, c].astype(BF16), sel_ref[...])
-            along_x = faces[c, :, 0:128].reshape(16, 2, 8, 128)
-            along_y = faces[c, :, 128:256].reshape(4, 4, 16, 128)
-            send_x[step, 0, c] = along_x[:, 1].reshape(128, 128).astype(BF16)
-            send_x[step, 1, c] = along_x[:, 0].reshape(128, 128).astype(BF16)
-            send_y[step, 0, c] = along_y[:, 3].reshape(64, 128).astype(BF16)
-            send_y[step, 1, c] = along_y[:, 0].reshape(64, 128).astype(BF16)
-        if step == 0:
+    loads[4].wait()
+    flights = {}
+
+    def emit(step, c):
+        faces[c] = dot(field[step % 2, c].astype(BF16), sel_ref[...])
+        along_x = faces[c, :, 0:128].reshape(16, 2, 8, 128)
+        along_y = faces[c, :, 128:256].reshape(4, 4, 16, 128)
+        send_x[step, 0, c] = packed_rows(along_x[:, 1].reshape(128, 128), True)
+        send_x[step, 1, c] = packed_rows(along_x[:, 0].reshape(128, 128), False)
+        send_y[step, 0, c] = packed_rows(along_y[:, 3].reshape(64, 128), True)
+        send_y[step, 1, c] = packed_rows(along_y[:, 0].reshape(64, 128), False)
+        if step == 0 and c == 0:
             pl.semaphore_wait(barrier, len(friends))
         copies = []
         for k, (src, dst, device) in enumerate(
             [
-                (send_x.at[step, 0], recv_x.at[step, 0], right),
-                (send_x.at[step, 1], recv_x.at[step, 1], left),
-                (send_y.at[step, 0], recv_y.at[step, 0], above),
-                (send_y.at[step, 1], recv_y.at[step, 1], below),
+                (send_x.at[step, 0, c], recv_x.at[step, 0, c], right),
+                (send_x.at[step, 1, c], recv_x.at[step, 1, c], left),
+                (send_y.at[step, 0, c], recv_y.at[step, 0, c], above),
+                (send_y.at[step, 1, c], recv_y.at[step, 1, c], below),
             ]
         ):
-            copy = remote(src, dst, halo_send.at[step, k], halo_recv.at[step, k], device)
+            copy = remote(
+                src, dst, halo_send.at[step, c, k], halo_recv.at[step, c, k], device
+            )
             copy.start()
             copies.append(copy)
+        flights[step, c] = copies
+
+    for c in range(3):
+        emit(0, c)
+    for copy in loads[5:7]:
+        copy.wait()
+    for step in range(STEPS):
+        now, later = step % 2, (step + 1) % 2
         for c in range(3):
             for row in range(0, 256, 128):
                 rows = slice(row, row + 128)
@@ -316,44 +336,46 @@
                     advect = advect + field[now, 1, rows, cols] * d_y
                     advect = advect + field[now, 2, rows, cols] * d_z
                     partial[c, rows, cols] = field[now, c, rows, cols] + (spread - advect)
-        for copy in copies:
-            copy.wait()
         for c in range(3):
+            for copy in flights[step, c]:
+                copy.wait()
             along_x = faces[c, :, 0:128].reshape(16, 2, 8, 128)
             along_y = faces[c, :, 128:256].reshape(4, 4, 16, 128)
             along_z = faces[c, :, 256:384].reshape(4, 8, 8, 128)
-            from_left = recv_x[step, 0, c].astype(F32).reshape(16, 1, 8, 128)
-            from_right = recv_x[step, 1, c].astype(F32).reshape(16, 1, 8, 128)
-            from_below = recv_y[step, 0, c].astype(F32).reshape(4, 1, 16, 128)
-            from_above = recv_y[step, 1, c].astype(F32).reshape(4, 1, 16, 128)
+            from_left = spread_rows(recv_x[step, 0, c]).reshape(16, 1, 8, 128)
+            from_right = spread_rows(recv_x[step, 1, c]).reshape(16, 1, 8, 128)
+            from_below = spread_rows(recv_y[step, 0, c]).reshape(4, 1, 16, 128)
+            from_above = spread_rows(recv_y[step, 1, c]).reshape(4, 1, 16, 128)
             from_below = jnp.where(grp > 0, from_below, 0.0)
             from_above = jnp.where(grp < 3, from_above, 0.0)
             before = jnp.concatenate([from_left, along_x[:, :1]], axis=1).reshape(256, 128)
             after = jnp.concatenate([along_x[:, 1:], from_right], axis=1).reshape(256, 128)
             low = lanes_low((256, 128))
-            beside_x = jnp.where(low, after, before).astype(BF16)
+            beside_x = swap_halves(jnp.where(low, after, before))
             before = jnp.concatenate([from_below, along_y[:, :3]], axis=1).reshape(256, 128)
             after = jnp.concatenate([along_y[:, 1:], from_above], axis=1).reshape(256, 128)
-            beside_y = jnp.where(low, after, before).astype(BF16)
+            beside_y = swap_halves(jnp.where(low, after, before))
             place = lax.broadcasted_iota(jnp.int32, (32, 8, 128), 1)
             flat_z = along_z.reshape(32, 8, 128)
             behind = jnp.concatenate([along_z[3:], along_z[:3]], axis=0).reshape(32, 8, 128)
             ahead = jnp.concatenate([along_z[1:], along_z[:1]], axis=0).reshape(32, 8, 128)
             before = pltpu.roll(jnp.where(place == 7, behind, flat_z), 1, 1).reshape(256, 128)
             after = pltpu.roll(jnp.where(place == 0, ahead, flat_z), 7, 1).reshape(256, 128)
-            beside_z = jnp.where(low, after, before).astype(BF16)
+            beside_z = swap_halves(jnp.where(low, after, before))
             beside = jnp.concatenate([beside_x, beside_y, beside_z], axis=1)
             for h in range(0, 512, 256):
                 cols = slice(h, h + 256)
-                pull = dot(beside, unsel_ref[:, cols])
+                pull = dot_cols(beside, sel_ref[cols])
                 field[later, c, :, cols] = (
                     partial[c, :, cols] + (TIME_STEP * VISCOSITY * PENALTY) * pull
                 )
+            if step + 1 < STEPS:
+                emit(step + 1, c)
 
     final = STEPS % 2
     snap_ref[:, 0:512] = field[final, 0].astype(BF16)
     snap_ref[:, 512:1024] = field[final, 2].astype(BF16)
-    for copy in loads[8:10]:
+    for copy in loads[7:9]:
         copy.wait()
 
     def block(index):
@@ -407,7 +429,7 @@
 
     for copy in h_copies:
         copy.wait()
-    for copy in loads[10:]:
+    for copy in loads[9:]:
         copy.wait()
     value = crop_h[...].reshape(256, 256).astype(F32)
     for dx, dz, moved in variants(value, 256):
@@ -597,7 +619,7 @@
             if which == 0:
                 tail[which] = spread_small(
                     [
-                        (small.at[peers_plane[d]], small_recv.at[d], dev_plane[d])
+                        (small.at[peers_depth[d]], small_recv.at[d], dev_depth[d])
                         for d in range(7)
                     ]
                 )
@@ -617,7 +639,7 @@
                 tail[which] = spread_small(triples)
         if phase == 1:
             if which == 0:
-                total = small[plane].astype(F32)
+                total = small[depth].astype(F32)
                 for d in range(7):
                     total = total + small_recv[d].astype(F32)
             else:
@@ -625,17 +647,19 @@
                 for d in range(15):
                     total = total + enc_recv[d].astype(F32)
             piece[...] = total.astype(BF16)
-            layers[depth] = piece[...]
+            place, devices = later_way[which]
+            layers[place] = piece[...]
             tail[which] = spread_small(
-                [(piece, layers.at[depth], dev_depth[d]) for d in range(7)]
+                [(piece, layers.at[place], devices[d]) for d in range(7)]
             )
         if phase == 2:
             total = layers[0].astype(F32)
             for d in range(1, 8):
                 total = total + layers[d].astype(F32)
-            ready[plane] = total.astype(BF16)
+            place, devices = later_way[1 - which]
+            ready[place] = total.astype(BF16)
             tail[which] = spread_small(
-                [(ready.at[plane], ready.at[plane], dev_plane[d]) for d in range(7)]
+                [(ready.at[place], ready.at[place], devices[d]) for d in range(7)]
             )
         if phase == 3:
             copy = pltpu.make_async_copy(
@@ -644,12 +668,13 @@
             copy.start()
             stores.append(copy)
 
+    later_way = ((plane, dev_plane), (depth, dev_depth))
     tails = (
         (small_piece, small_layers, small_ready),
         (enc_piece, enc_layers, enc_ready),
     )
 
-    for part in range(PARTS):
+    for part in (1, 2, 0):
         conv_grad(part)
         advance(part, 0)
     conv_grad(PARTS)
@@ -693,9 +718,9 @@
 
 
 ORDER = [
-    (1, 1), (0, 1), (2, 1), (3, 1), (4, 1),
-    (1, 2), (0, 2), (2, 2), (3, 2), (4, 2),
-    (1, 3), (0, 3), (2, 3), (3, 3), (4, 3),
+    (1, 1), (3, 1), (2, 1), (0, 1), (4, 1),
+    (1, 2), (3, 2), (0, 2), (2, 2), (4, 2),
+    (1, 3), (0, 3), (2, 3), (4, 3), (3, 3),
     (1, 4), (0, 4), (2, 4),
 ]
 
@@ -719,8 +744,9 @@
     load_sem,
     store_sem,
 ):
-    pairs = [(result_hbm.at[part], result.at[part]) for part in range(PARTS)]
-    pairs += [(small_hbm, small), (enc_grad_hbm, enc_grad), (vel_in, vel_ref)]
+    pairs = [(vel_in.at[c], vel_ref.at[c]) for c in range(3)]
+    pairs += [(result_hbm.at[part], result.at[part]) for part in range(PARTS)]
+    pairs += [(small_hbm, small), (enc_grad_hbm, enc_grad)]
     loads = [
         pltpu.make_async_copy(src, dst, load_sem.at[k]) for k, (src, dst) in enumerate(pairs)
     ]
@@ -733,15 +759,18 @@
         copy.start()
         stores.append(copy)
 
+    for c in range(3):
+        loads[c].wait()
+        store(vel_ref.at[c], vel_out.at[c])
     for part in range(PARTS):
-        loads[part].wait()
+        loads[3 + part].wait()
         for half in range(2):
             lanes = slice(128 * half, 128 * half + 128)
             value = result[part, 32 * half : 32 * half + 32].astype(F32)
             conv_ref[512 * part : 512 * part + 512, lanes] = value.reshape(512, 128)
         span = pl.ds(512 * part, 512)
         store(conv_ref.at[span], conv_hbm.at[span])
-    loads[PARTS].wait()
+    loads[3 + PARTS].wait()
     for half in range(2):
         lanes = slice(128 * half, 128 * half + 128)
         value = small[3 * half : 3 * half + 3].astype(F32).reshape(192, 128)
@@ -750,12 +779,10 @@
     store(conv_ref.at[span], conv_hbm.at[span])
     head_ref[...] = small[6].astype(F32).reshape(64, 128)
     store(head_ref, head_hbm)
-    loads[PARTS + 1].wait()
+    loads[4 + PARTS].wait()
     for b in range(8):
         enc_ref[:, 128 * b : 128 * b + 128] = enc_grad[b].astype(F32)
     store(enc_ref, enc_hbm)
-    loads[PARTS + 2].wait()
-    store(vel_ref, vel_out)
     for copy in stores:
         copy.wait()
 
@@ -798,12 +825,12 @@
             vm((2, 3, 256, 512), F32),
             vm((3, 256, 512), F32),
             vm((3, 256, 384), F32),
-            vm((STEPS, 2, 3, 128, 128), BF16),
             vm((STEPS, 2, 3, 64, 128), BF16),
-            vm((STEPS, 2, 3, 128, 128), BF16),
+            vm((STEPS, 2, 3, 32, 128), BF16),
             vm((STEPS, 2, 3, 64, 128), BF16),
-            dma((STEPS, 4)),
-            dma((STEPS, 4)),
+            vm((STEPS, 2, 3, 32, 128), BF16),
+            dma((STEPS, 3, 4)),
+            dma((STEPS, 3, 4)),
             vm((4, 64, 256), BF16),
             vm((256, 256), F32),
             vm((256, 1024), BF16),
@@ -868,8 +895,8 @@
             vm((CONV_ROWS, 256), F32),
             vm((64, 1024), F32),
             vm((64, 128), F32),
-            dma((PARTS + 3,)),
-            dma((PARTS + 4,)),
+            dma((PARTS + 5,)),
+            dma((PARTS + 6,)),
         ],
         compiler_params=pltpu.CompilerParams(vmem_limit_bytes=62 * 2**20),
     )(result, small, enc_grad, velocity_next)

time: 74.2 us -> 75 us (1.011)
  Pallas kernels: 71.9 us -> 72.9 us
    pallas_call x1, Pallas kernels: 68.9 us -> 69.9 us  [body(): pl.pallas_call(lambda *refs: step_kernel(lax.axis_size('sim'), *refs), na...]
where the time goes in v5:
time: 75 us; the launch traced here: 73.7 us
  Pallas kernels  72.9 us (97%)
  between operations  0.8 us (1%)
    pallas_call x1, Pallas kernels, body(): pl.pallas_call(lambda *refs: step_kernel(lax.axis_size('sim'), *refs), na...  69.9 us
    pallas_call x1, Pallas kernels, body(): pl.pallas_call(finish_kernel, name='finish', out_shape=(shaped((CONV_ROWS...  3 us

profile of v5, /device:TPU:24, one launch (start us, length us, event | category | flops | bytes accessed | tf_op | source)
XLA Modules:
  0.0 73.7 jit_solution(18158732049554380187)
XLA Ops:
  0.6 69.9 %step.1 = (f32[3,256,512]{2,1,0:T(8,128)}, bf16[3,64,16,128]{3,2,1,0:T(8,128)(2,1)}, bf16[8,4,16,128]{3,2,1,0:T(8,128)(2,1)}, bf16[8,64,128]{2,1,0:T(8,128)(2,1)}) custom-call(f32[3,256,512]{2,1,0:T(8,128)} %bitcast.7, s32[1,256]{1,0:T(1,128)} %bitcast.8, bf16[512,1024]{1,0:T(8,128)(2,1)} %constant.8.clone.refs_2_, bf16[256,512]{1,0:T(8,128)(2,1)} %constant.9.clone.refs_3_, ...), custom_call_target="tpu_custom_call" | custom-call | tf_op jit(solution)/shard_map/step/pallas_call | solution.py:803
  70.5 3.0 %finish.1 = (f32[1728,256]{1,0:T(8,128)}, f32[64,1024]{1,0:T(8,128)}, f32[64,128]{1,0:T(8,128)}, f32[3,256,512]{2,1,0:T(8,128)}) custom-call(bf16[3,64,16,128]{3,2,1,0:T(8,128)(2,1)} %get-tuple-element.12.result_hbm, bf16[8,4,16,128]{3,2,1,0:T(8,128)(2,1)} %get-tuple-element.13.small_hbm, bf16[8,64,128]{2,1,0:T(8,128)(2,1)} %get-tuple-element.14.enc_grad_hbm, ...), custom_call_target="tpu_custom_call" | custom-call | tf_op jit(solution)/shard_map/finish/pallas_call | solution.py:879

commit v6 on v5

--- a/solution.py
+++ b/solution.py
@@ -316,6 +316,43 @@
             copies.append(copy)
         flights[step, c] = copies
 
+    def close(step, c):
+        now, later = step % 2, (step + 1) % 2
+        for copy in flights[step, c]:
+            copy.wait()
+        along_x = faces[c, :, 0:128].reshape(16, 2, 8, 128)
+        along_y = faces[c, :, 128:256].reshape(4, 4, 16, 128)
+        along_z = faces[c, :, 256:384].reshape(4, 8, 8, 128)
+        from_left = spread_rows(recv_x[step, 0, c]).reshape(16, 1, 8, 128)
+        from_right = spread_rows(recv_x[step, 1, c]).reshape(16, 1, 8, 128)
+        from_below = spread_rows(recv_y[step, 0, c]).reshape(4, 1, 16, 128)
+        from_above = spread_rows(recv_y[step, 1, c]).reshape(4, 1, 16, 128)
+        from_below = jnp.where(grp > 0, from_below, 0.0)
+        from_above = jnp.where(grp < 3, from_above, 0.0)
+        before = jnp.concatenate([from_left, along_x[:, :1]], axis=1).reshape(256, 128)
+        after = jnp.concatenate([along_x[:, 1:], from_right], axis=1).reshape(256, 128)
+        low = lanes_low((256, 128))
+        beside_x = swap_halves(jnp.where(low, after, before))
+        before = jnp.concatenate([from_below, along_y[:, :3]], axis=1).reshape(256, 128)
+        after = jnp.concatenate([along_y[:, 1:], from_above], axis=1).reshape(256, 128)
+        beside_y = swap_halves(jnp.where(low, after, before))
+        place = lax.broadcasted_iota(jnp.int32, (32, 8, 128), 1)
+        flat_z = along_z.reshape(32, 8, 128)
+        behind = jnp.concatenate([along_z[3:], along_z[:3]], axis=0).reshape(32, 8, 128)
+        ahead = jnp.concatenate([along_z[1:], along_z[:1]], axis=0).reshape(32, 8, 128)
+        before = pltpu.roll(jnp.where(place == 7, behind, flat_z), 1, 1).reshape(256, 128)
+        after = pltpu.roll(jnp.where(place == 0, ahead, flat_z), 7, 1).reshape(256, 128)
+        beside_z = swap_halves(jnp.where(low, after, before))
+        beside = jnp.concatenate([beside_x, beside_y, beside_z], axis=1)
+        for h in range(0, 512, 256):
+            cols = slice(h, h + 256)
+            pull = dot_cols(beside, sel_ref[cols])
+            field[later, c, :, cols] = (
+                partial[c, :, cols] + (TIME_STEP * VISCOSITY * PENALTY) * pull
+            )
+        if step + 1 < STEPS:
+            emit(step + 1, c)
+
     for c in range(3):
         emit(0, c)
     for copy in loads[5:7]:
@@ -336,41 +373,8 @@
                     advect = advect + field[now, 1, rows, cols] * d_y
                     advect = advect + field[now, 2, rows, cols] * d_z
                     partial[c, rows, cols] = field[now, c, rows, cols] + (spread - advect)
-        for c in range(3):
-            for copy in flights[step, c]:
-                copy.wait()
-            along_x = faces[c, :, 0:128].reshape(16, 2, 8, 128)
-            along_y = faces[c, :, 128:256].reshape(4, 4, 16, 128)
-            along_z = faces[c, :, 256:384].reshape(4, 8, 8, 128)
-            from_left = spread_rows(recv_x[step, 0, c]).reshape(16, 1, 8, 128)
-            from_right = spread_rows(recv_x[step, 1, c]).reshape(16, 1, 8, 128)
-            from_below = spread_rows(recv_y[step, 0, c]).reshape(4, 1, 16, 128)
-            from_above = spread_rows(recv_y[step, 1, c]).reshape(4, 1, 16, 128)
-            from_below = jnp.where(grp > 0, from_below, 0.0)
-            from_above = jnp.where(grp < 3, from_above, 0.0)
-            before = jnp.concatenate([from_left, along_x[:, :1]], axis=1).reshape(256, 128)
-            after = jnp.concatenate([along_x[:, 1:], from_right], axis=1).reshape(256, 128)
-            low = lanes_low((256, 128))
-            beside_x = swap_halves(jnp.where(low, after, before))
-            before = jnp.concatenate([from_below, along_y[:, :3]], axis=1).reshape(256, 128)
-            after = jnp.concatenate([along_y[:, 1:], from_above], axis=1).reshape(256, 128)
-            beside_y = swap_halves(jnp.where(low, after, before))
-            place = lax.broadcasted_iota(jnp.int32, (32, 8, 128), 1)
-            flat_z = along_z.reshape(32, 8, 128)
-            behind = jnp.concatenate([along_z[3:], along_z[:3]], axis=0).reshape(32, 8, 128)
-            ahead = jnp.concatenate([along_z[1:], along_z[:1]], axis=0).reshape(32, 8, 128)
-            before = pltpu.roll(jnp.where(place == 7, behind, flat_z), 1, 1).reshape(256, 128)
-            after = pltpu.roll(jnp.where(place == 0, ahead, flat_z), 7, 1).reshape(256, 128)
-            beside_z = swap_halves(jnp.where(low, after, before))
-            beside = jnp.concatenate([beside_x, beside_y, beside_z], axis=1)
-            for h in range(0, 512, 256):
-                cols = slice(h, h + 256)
-                pull = dot_cols(beside, sel_ref[cols])
-                field[later, c, :, cols] = (
-                    partial[c, :, cols] + (TIME_STEP * VISCOSITY * PENALTY) * pull
-                )
-            if step + 1 < STEPS:
-                emit(step + 1, c)
+        for c in (0, 2, 1) if step + 1 < STEPS else (0, 2):
+            close(step, c)
 
     final = STEPS % 2
     snap_ref[:, 0:512] = field[final, 0].astype(BF16)
@@ -393,6 +397,7 @@
     z1_ref[...] = z1
     h1_ref[...] = (z1 * jax.nn.sigmoid(z1)).astype(BF16).reshape(4, 64, 256)
     h_copies = exchange(0, [(h1_ref.at[p], crop_h.at[grp]) for p in peers])
+    close(STEPS - 1, 1)
     table_high, table_low = parts(bottom_ref[...])
     stress = []
     for c in (0, 2):
@@ -619,7 +624,7 @@
             if which == 0:
                 tail[which] = spread_small(
                     [
-                        (small.at[peers_depth[d]], small_recv.at[d], dev_depth[d])
+                        (small.at[peers_plane[d]], small_recv.at[d], dev_plane[d])
                         for d in range(7)
                     ]
                 )
@@ -639,7 +644,7 @@
                 tail[which] = spread_small(triples)
         if phase == 1:
             if which == 0:
-                total = small[depth].astype(F32)
+                total = small[plane].astype(F32)
                 for d in range(7):
                     total = total + small_recv[d].astype(F32)
             else:
@@ -647,7 +652,7 @@
                 for d in range(15):
                     total = total + enc_recv[d].astype(F32)
             piece[...] = total.astype(BF16)
-            place, devices = later_way[which]
+            place, devices = depth, dev_depth
             layers[place] = piece[...]
             tail[which] = spread_small(
                 [(piece, layers.at[place], devices[d]) for d in range(7)]
@@ -656,7 +661,7 @@
             total = layers[0].astype(F32)
             for d in range(1, 8):
                 total = total + layers[d].astype(F32)
-            place, devices = later_way[1 - which]
+            place, devices = plane, dev_plane
             ready[place] = total.astype(BF16)
             tail[which] = spread_small(
                 [(ready.at[place], ready.at[place], devices[d]) for d in range(7)]
@@ -668,13 +673,12 @@
             copy.start()
             stores.append(copy)
 
-    later_way = ((plane, dev_plane), (depth, dev_depth))
     tails = (
         (small_piece, small_layers, small_ready),
         (enc_piece, enc_layers, enc_ready),
     )
 
-    for part in (1, 2, 0):
+    for part in (0, 1, 2):
         conv_grad(part)
         advance(part, 0)
     conv_grad(PARTS)
@@ -718,9 +722,9 @@
 
 
 ORDER = [
-    (1, 1), (3, 1), (2, 1), (0, 1), (4, 1),
-    (1, 2), (3, 2), (0, 2), (2, 2), (4, 2),
-    (1, 3), (0, 3), (2, 3), (4, 3), (3, 3),
+    (1, 1), (0, 1), (2, 1), (3, 1), (4, 1),
+    (1, 2), (0, 2), (2, 2), (3, 2), (4, 2),
+    (1, 3), (0, 3), (2, 3), (3, 3), (4, 3),
     (1, 4), (0, 4), (2, 4),
 ]
 

time: 75 us -> 72 us (0.960)
  Pallas kernels: 72.9 us -> 70.2 us
    pallas_call x1, Pallas kernels: 69.9 us -> 67.2 us  [body(): pl.pallas_call(lambda *refs: step_kernel(lax.axis_size('sim'), *refs), na...]
where the time goes in v6:
time: 72 us; the launch traced here: 71 us
  Pallas kernels  70.2 us (98%)
  between operations  0.8 us (1%)
    pallas_call x1, Pallas kernels, body(): pl.pallas_call(lambda *refs: step_kernel(lax.axis_size('sim'), *refs), na...  67.2 us
    pallas_call x1, Pallas kernels, body(): pl.pallas_call(finish_kernel, name='finish', out_shape=(shaped((CONV_ROWS...  3 us

profile of v6, /device:TPU:24, one launch (start us, length us, event | category | flops | bytes accessed | tf_op | source)
XLA Modules:
  0.0 71.0 jit_solution(8369270774889764444)
XLA Ops:
  0.6 67.2 %step.1 = (f32[3,256,512]{2,1,0:T(8,128)}, bf16[3,64,16,128]{3,2,1,0:T(8,128)(2,1)}, bf16[8,4,16,128]{3,2,1,0:T(8,128)(2,1)}, bf16[8,64,128]{2,1,0:T(8,128)(2,1)}) custom-call(f32[3,256,512]{2,1,0:T(8,128)} %bitcast.7, s32[1,256]{1,0:T(1,128)} %bitcast.8, bf16[512,1024]{1,0:T(8,128)(2,1)} %constant.8.clone.refs_2_, bf16[256,512]{1,0:T(8,128)(2,1)} %constant.9.clone.refs_3_, ...), custom_call_target="tpu_custom_call" | custom-call | tf_op jit(solution)/shard_map/step/pallas_call | solution.py:807
  67.8 3.0 %finish.1 = (f32[1728,256]{1,0:T(8,128)}, f32[64,1024]{1,0:T(8,128)}, f32[64,128]{1,0:T(8,128)}, f32[3,256,512]{2,1,0:T(8,128)}) custom-call(bf16[3,64,16,128]{3,2,1,0:T(8,128)(2,1)} %get-tuple-element.12.result_hbm, bf16[8,4,16,128]{3,2,1,0:T(8,128)(2,1)} %get-tuple-element.13.small_hbm, bf16[8,64,128]{2,1,0:T(8,128)(2,1)} %get-tuple-element.14.enc_grad_hbm, ...), custom_call_target="tpu_custom_call" | custom-call | tf_op jit(solution)/shard_map/finish/pallas_call | solution.py:883

commit v7 on v6

--- a/solution.py
+++ b/solution.py
@@ -550,7 +550,7 @@
 
     depth_way = (depth, peers_depth, dev_depth)
     plane_way = (plane, peers_plane, dev_plane)
-    ways = [(depth_way, plane_way)] + [(plane_way, depth_way)] * 2
+    ways = [(plane_way, depth_way)] * 3
     flying = {}
 
     def eight(index):
@@ -722,10 +722,10 @@
 
 
 ORDER = [
-    (1, 1), (0, 1), (2, 1), (3, 1), (4, 1),
-    (1, 2), (0, 2), (2, 2), (3, 2), (4, 2),
-    (1, 3), (0, 3), (2, 3), (3, 3), (4, 3),
-    (1, 4), (0, 4), (2, 4),
+    (0, 1), (1, 1), (2, 1), (3, 1), (4, 1),
+    (0, 2), (1, 2), (2, 2), (3, 2), (4, 2),
+    (0, 3), (1, 3), (2, 3), (3, 3), (4, 3),
+    (0, 4), (1, 4), (2, 4),
 ]
 
 

time: 72 us -> 75.8 us (1.053)
  Pallas kernels: 70.2 us -> 74.5 us
    pallas_call x1, Pallas kernels: 67.2 us -> 71.5 us  [body(): pl.pallas_call(lambda *refs: step_kernel(lax.axis_size('sim'), *refs), na...]
where the time goes in v7:
time: 75.8 us; the launch traced here: 75.3 us
  Pallas kernels  74.5 us (98%)
  between operations  0.8 us (1%)
    pallas_call x1, Pallas kernels, body(): pl.pallas_call(lambda *refs: step_kernel(lax.axis_size('sim'), *refs), na...  71.5 us
    pallas_call x1, Pallas kernels, body(): pl.pallas_call(finish_kernel, name='finish', out_shape=(shaped((CONV_ROWS...  3 us

profile of v7, /device:TPU:24, one launch (start us, length us, event | category | flops | bytes accessed | tf_op | source)
XLA Modules:
  0.0 75.3 jit_solution(14294371661516875045)
XLA Ops:
  0.6 71.5 %step.1 = (f32[3,256,512]{2,1,0:T(8,128)}, bf16[3,64,16,128]{3,2,1,0:T(8,128)(2,1)}, bf16[8,4,16,128]{3,2,1,0:T(8,128)(2,1)}, bf16[8,64,128]{2,1,0:T(8,128)(2,1)}) custom-call(f32[3,256,512]{2,1,0:T(8,128)} %bitcast.7, s32[1,256]{1,0:T(1,128)} %bitcast.8, bf16[512,1024]{1,0:T(8,128)(2,1)} %constant.8.clone.refs_2_, bf16[256,512]{1,0:T(8,128)(2,1)} %constant.9.clone.refs_3_, ...), custom_call_target="tpu_custom_call" | custom-call | tf_op jit(solution)/shard_map/step/pallas_call | solution.py:807
  72.1 3.0 %finish.1 = (f32[1728,256]{1,0:T(8,128)}, f32[64,1024]{1,0:T(8,128)}, f32[64,128]{1,0:T(8,128)}, f32[3,256,512]{2,1,0:T(8,128)}) custom-call(bf16[3,64,16,128]{3,2,1,0:T(8,128)(2,1)} %get-tuple-element.12.result_hbm, bf16[8,4,16,128]{3,2,1,0:T(8,128)(2,1)} %get-tuple-element.13.small_hbm, bf16[8,64,128]{2,1,0:T(8,128)(2,1)} %get-tuple-element.14.enc_grad_hbm, ...), custom_call_target="tpu_custom_call" | custom-call | tf_op jit(solution)/shard_map/finish/pallas_call | solution.py:883
